TPU v7x, 32 devices: a whole 2x2x4 slice. The times are simulated.
32 devices in a mesh: ctx: 8 (over z, y), ch: 4 (over x, core).
Axes of the slice: x: 2, y: 2, z: 4, core: 2. Of those that a mesh axis runs over, the one named last changes fastest.
Arguments:
- queries: bfloat16 [2048, 4096], P('ctx', 'ch'), may hold values from -6 to 6
- keys: bfloat16 [2048, 4096], P('ctx', 'ch'), may hold values from -6 to 6
- values: bfloat16 [2048, 4096], P('ctx', 'ch'), may hold values from -6 to 6
- long_filter: float32 [2048, 4096], P('ctx', 'ch'), may hold values from -1.05 to 1.05
- short_filters: float32 [3, 3, 4096], P(None, None, 'ch'), may hold values from -3.6 to 3.6
- skip: float32 [4096], P('ch'), may hold values from -1 to 1
- w_out: bfloat16 [4096, 8192], P('ch'), may hold values from -0.09375 to 0.09375
- d_out: bfloat16 [2048, 8192], P('ctx', 'ch'), may hold values from -6 to 6
Outputs:
- d_queries: bfloat16 [2048, 4096], P('ctx', 'ch')
- d_keys: bfloat16 [2048, 4096], P('ctx', 'ch')
- d_values: bfloat16 [2048, 4096], P('ctx', 'ch')
- d_long: float32 [2048, 4096], P('ctx', 'ch')
- d_short: float32 [3, 3, 4096], P(None, None, 'ch')
- d_skip: float32 [4096], P('ch')
All inputs are finite; a program needn't handle non-finite values.
Results may differ from a plain program's by a relative error of at most 0.0049.
Values may be sent and summed in bfloat16 or wider, within the bound.
A program may use at most 128 MiB of HBM per device.

v0:
```python
import math

import jax
import jax.numpy as jnp
from jax import lax
from jax.sharding import PartitionSpec as P


def passed_along(block, axis, distance):
    devices = range(lax.axis_size(axis))
    route = [(i - distance, i) for i in devices if i - distance in devices]
    return lax.ppermute(block, axis, route)


def phases(left_index, right_index, modulus):
    product = left_index[:, None] * right_index[None, :] % modulus
    angle = product.astype(jnp.float32) * (2.0 * math.pi / modulus)
    return (jnp.cos(angle), jnp.sin(angle))


def mat_apply(table, data, form):
    return jnp.einsum(form, table, data, precision=lax.Precision.HIGHEST)


def fine_forward(fine_cos, fine_sin, real_part, imag_part):
    spec_real = mat_apply(fine_cos, real_part, "kb,sbc->skc") + mat_apply(
        fine_sin, imag_part, "kb,sbc->skc"
    )
    spec_imag = mat_apply(fine_cos, imag_part, "kb,sbc->skc") - mat_apply(
        fine_sin, real_part, "kb,sbc->skc"
    )
    return (spec_real, spec_imag)


def fine_inverse(fine_cos, fine_sin, real_part, imag_part):
    back_real = mat_apply(fine_cos, real_part, "bk,skc->sbc") - mat_apply(
        fine_sin, imag_part, "bk,skc->sbc"
    )
    back_imag = mat_apply(fine_cos, imag_part, "bk,skc->sbc") + mat_apply(
        fine_sin, real_part, "bk,skc->sbc"
    )
    return (back_real, back_imag)


def forward_half(regrouped, ctx_size, position, block_len, total_len):
    seq_rows = ctx_size * block_len
    coarse = jnp.arange(ctx_size, dtype=jnp.int32)
    coarse_cos, coarse_sin = phases(coarse, coarse, 2 * ctx_size)
    signs = 1.0 - 2.0 * (coarse % 2).astype(jnp.float32)
    first_row = (coarse == 0)[:, None]
    coef_real = jnp.where(first_row, jnp.float32(1.0), coarse_cos)
    coef_imag = jnp.where(first_row, signs[None, :], -coarse_sin)
    first_real = mat_apply(coef_real, regrouped, "ka,sabc->skbc")
    first_imag = mat_apply(coef_imag, regrouped, "ka,sabc->skbc")
    fine_global = position * block_len + jnp.arange(block_len, dtype=jnp.int32)
    twist_cos, twist_sin = phases(coarse, fine_global, total_len)
    twist_cos = twist_cos[None, :, :, None]
    twist_sin = twist_sin[None, :, :, None]
    second_real = first_real * twist_cos + first_imag * twist_sin
    second_imag = first_imag * twist_cos - first_real * twist_sin
    moved = lax.all_to_all(
        jnp.stack([second_real, second_imag], axis=1),
        "ctx",
        split_axis=2,
        concat_axis=3,
        tiled=True,
    )
    packed_real = moved[:, 0, 0]
    packed_imag = moved[:, 1, 0]
    fine_index = jnp.arange(seq_rows, dtype=jnp.int32)
    fine_cos, fine_sin = phases(fine_index, fine_index, seq_rows)
    shift_cos, shift_sin = phases(fine_index, jnp.ones((1,), jnp.int32), 2 * seq_rows)
    shift_cos = shift_cos[None]
    shift_sin = shift_sin[None]

    def corner_slots(operands):
        low_part, top_part = operands
        main_real, main_imag = fine_forward(fine_cos, fine_sin, low_part, jnp.zeros_like(low_part))
        top_real, top_imag = fine_forward(
            fine_cos, fine_sin, top_part * shift_cos, -top_part * shift_sin
        )
        return (jnp.stack([main_real, top_real], axis=1), jnp.stack([main_imag, top_imag], axis=1))

    def plain_slots(operands):
        real_part, imag_part = operands
        main_real, main_imag = fine_forward(fine_cos, fine_sin, real_part, imag_part)
        empty = jnp.zeros_like(main_real)
        return (jnp.stack([main_real, empty], axis=1), jnp.stack([main_imag, empty], axis=1))

    return lax.cond(position == 0, corner_slots, plain_slots, (packed_real, packed_imag))


def inverse_half(spec_real, spec_imag, ctx_size, position, block_len, total_len):
    seq_rows = spec_real.shape[2]
    fine_index = jnp.arange(seq_rows, dtype=jnp.int32)
    fine_cos, fine_sin = phases(fine_index, fine_index, seq_rows)
    shift_cos, shift_sin = phases(fine_index, jnp.ones((1,), jnp.int32), 2 * seq_rows)
    shift_cos = shift_cos[None]
    shift_sin = shift_sin[None]

    def corner_back(operands):
        slot_real, slot_imag = operands
        low_real, low_imag = fine_inverse(fine_cos, fine_sin, slot_real[:, 0], slot_imag[:, 0])
        top_real, top_imag = fine_inverse(fine_cos, fine_sin, slot_real[:, 1], slot_imag[:, 1])
        return (low_real, top_real * shift_cos - top_imag * shift_sin)

    def plain_back(operands):
        slot_real, slot_imag = operands
        return fine_inverse(fine_cos, fine_sin, slot_real[:, 0], slot_imag[:, 0])

    back_real, back_imag = lax.cond(position == 0, corner_back, plain_back, (spec_real, spec_imag))
    sending = jnp.stack([back_real, back_imag], axis=1)[:, :, None]
    returned = lax.all_to_all(sending, "ctx", split_axis=3, concat_axis=2, tiled=True)
    part_real = returned[:, 0]
    part_imag = returned[:, 1]
    coarse = jnp.arange(ctx_size, dtype=jnp.int32)
    fine_global = position * block_len + jnp.arange(block_len, dtype=jnp.int32)
    twist_cos, twist_sin = phases(coarse, fine_global, total_len)
    twist_cos = twist_cos[None, :, :, None]
    twist_sin = twist_sin[None, :, :, None]
    turned_real = part_real * twist_cos - part_imag * twist_sin
    turned_imag = part_imag * twist_cos + part_real * twist_sin
    coarse_cos, coarse_sin = phases(coarse, coarse, 2 * ctx_size)
    signs = 1.0 - 2.0 * (coarse % 2).astype(jnp.float32)
    first_col = (coarse == 0)[None, :]
    coef_real = jnp.where(first_col, jnp.float32(1.0), 2.0 * coarse_cos)
    coef_imag = jnp.where(first_col, signs[:, None], -2.0 * coarse_sin)
    result = mat_apply(coef_real, turned_real, "ak,skbc->sabc") + mat_apply(
        coef_imag, turned_imag, "ak,skbc->sabc"
    )
    return result / total_len


def per_device(queries, keys, values, long_filter, short_filters, skip, w_out, d_out):
    ctx_size = lax.axis_size("ctx")
    position = lax.axis_index("ctx")
    seq_rows = queries.shape[0]
    width = queries.shape[1]
    block_len = seq_rows // ctx_size
    total_len = 2 * ctx_size * seq_rows
    tap_count = short_filters.shape[1]
    rim_width = tap_count - 1
    streams = jnp.stack([queries, keys, values])
    before = passed_along(streams[:, seq_rows - rim_width :, :], "ctx", 1)
    extended = jnp.concatenate([before, streams], axis=1).astype(jnp.float32)
    filtered = jnp.zeros((3, seq_rows, width), jnp.float32)
    for j in range(tap_count):
        filtered = (
            filtered
            + short_filters[:, j, None, :]
            * extended[:, rim_width - j : rim_width - j + seq_rows, :]
        )
    mixed = filtered[1] * filtered[2]
    accumulated = lax.dot_general(
        lax.all_gather(d_out, "ch", axis=1, tiled=True),
        w_out,
        (((1,), (1,)), ((), ())),
        preferred_element_type=jnp.float32,
    )
    grad_o = lax.optimization_barrier(accumulated.astype(jnp.bfloat16)).astype(jnp.float32)
    grad_y = grad_o * filtered[0]
    signals = jnp.stack([mixed, long_filter, grad_y])
    regrouped = lax.all_to_all(signals[:, None], "ctx", split_axis=2, concat_axis=1, tiled=True)
    spec_real, spec_imag = forward_half(regrouped, ctx_size, position, block_len, total_len)
    mix_re, mix_im = (spec_real[0], spec_imag[0])
    fil_re, fil_im = (spec_real[1], spec_imag[1])
    grad_re, grad_im = (spec_real[2], spec_imag[2])
    out_re = mix_re * fil_re - mix_im * fil_im
    out_im = mix_re * fil_im + mix_im * fil_re
    back_re = grad_re * fil_re + grad_im * fil_im
    back_im = grad_im * fil_re - grad_re * fil_im
    corr_re = grad_re * mix_re + grad_im * mix_im
    corr_im = grad_im * mix_re - grad_re * mix_im
    fields = inverse_half(
        jnp.stack([out_re, back_re, corr_re]),
        jnp.stack([out_im, back_im, corr_im]),
        ctx_size,
        position,
        block_len,
        total_len,
    )
    timed = lax.all_to_all(fields, "ctx", split_axis=1, concat_axis=2, tiled=True).reshape(
        3, seq_rows, width
    )
    conv_y = timed[0]
    conv_back = timed[1]
    d_long = timed[2]
    y_full = conv_y + skip[None, :] * mixed
    grad_mixed = conv_back + skip[None, :] * grad_y
    grads = jnp.stack([grad_o * y_full, grad_mixed * filtered[2], grad_mixed * filtered[1]])
    after = passed_along(grads[:, :rim_width, :], "ctx", -1)
    grads_ext = jnp.concatenate([grads, after], axis=1)
    stream_grads = jnp.zeros((3, seq_rows, width), jnp.float32)
    tap_terms = []
    for j in range(tap_count):
        stream_grads = (
            stream_grads + short_filters[:, j, None, :] * grads_ext[:, j : j + seq_rows, :]
        )
        tap_terms.append(
            jnp.sum(grads * extended[:, rim_width - j : rim_width - j + seq_rows, :], axis=1)
        )
    short_terms = jnp.stack(tap_terms, axis=1)
    skip_term = jnp.sum(grad_y * mixed, axis=0)
    d_short, d_skip = lax.psum((short_terms, skip_term), "ctx")
    return (
        stream_grads[0].astype(jnp.bfloat16),
        stream_grads[1].astype(jnp.bfloat16),
        stream_grads[2].astype(jnp.bfloat16),
        d_long,
        d_short,
        d_skip,
    )


def solution(mesh):
    in_specs = (
        P("ctx", "ch"),
        P("ctx", "ch"),
        P("ctx", "ch"),
        P("ctx", "ch"),
        P(None, None, "ch"),
        P("ch"),
        P("ch", None),
        P("ctx", "ch"),
    )
    out_specs = (
        P("ctx", "ch"),
        P("ctx", "ch"),
        P("ctx", "ch"),
        P("ctx", "ch"),
        P(None, None, "ch"),
        P("ch"),
    )
    return jax.shard_map(
        per_device, mesh=mesh, in_specs=in_specs, out_specs=out_specs, check_vma=False
    )
```

profile of v0, /device:TPU:0, one launch (start us, length us, event | category | flops | bytes accessed | tf_op | source)
XLA Modules:
  0.0 732.7 jit_solution(4294775864192392248)
XLA Ops:
  8.7 4.9 collective-permute-start
  18.4 28.4 %all-gather.2.cloned.1.call-done = bf16[256,8192]{1,0:T(8,128)(2,1)} async-done(((bf16[256,2048]{1,0:T(8,128)(2,1)}), bf16[256,8192]{1,0:T(8,128)(2,1)}) %all-gather.2.cloned.1.call-update) | async-done | bytes 4194320 | tf_op jit(solution)/shard_map/all_gather | solution.py:155
  46.8 12.4 %convolution_convert_fusion = bf16[256,1024]{1,0:T(8,128)(2,1)} fusion(bf16[256,8192]{1,0:T(8,128)(2,1)} %all-gather.2.cloned.1.call-done, bf16[1024,8192]{1,0:T(8,128)(2,1)} %param.18), kind=kOutput, calls=%fused_computation.137 | convolution fusion | flops 4295229440 | bytes 21495808 | tf_op jit(solution)/shard_map/dot_general | solution.py:154
  61.2 4.9 copy.66
  66.1 5.7 all-to-all-start
  72.0 70.8 %all-to-all-done = f32[3,1,256,1024]{3,1,0,2:T(1,128)S(1)} async-done(((f32[3,1,256,1024]{3,1,0,2:T(1,128)}), f32[3,1,256,1024]{3,1,0,2:T(1,128)S(1)}, u32[]{:S(2)}, u32[]{:S(2)}) %all-to-all-start) | async-done | bytes 3145760 | tf_op jit(solution)/shard_map/all_to_all | solution.py:163
  143.5 5.6 fusion.93
  149.1 6.2 fusion.82
  156.6 6.3 copy.70
  168.9 136.6 %all-to-all-done.1 = f32[3,2,8,32,1024]{4,3,0,1,2:T(8,128)} async-done(((f32[3,2,8,32,1024]{4,3,0,1,2:T(8,128)}), f32[3,2,8,32,1024]{4,3,0,1,2:T(8,128)}, u32[]{:S(2)}, u32[]{:S(2)}) %all-to-all-start.1) | async-done | bytes 6291488 | tf_op jit(solution)/shard_map/all_to_all | solution.py:61
  310.0 48.2 %conditional.2 = ((f32[3,2,256,1024]{2,3,0,1:T(8,128)}, f32[3,2,256,1024]{2,3,0,1:T(8,128)})) conditional(s32[]{:T(128)} %convert_element_type.132, (f32[3,256,1024]{2,1,0:T(8,128)S(1)}, f32[256,256]{1,0:T(8,128)S(1)}, f32[3,256,1024]{2,1,0:T(8,128)S(1)}, f32[256,256]{1,0:T(8,128)S(1)}, f32[256,256]{1,0:T(8,128)S(1)}, ...), branch_computations={%region_0.1_spmd.clone, %region_1.2_spmd.clone} | conditional | flops 19338362880 | bytes 130027672 | solution.py:90
  335.6 5.7 fusion.74
  346.6 5.8 subtract_bitcast_fusion.5
  352.4 5.4 pad_maximum_fusion
  358.2 7.8 %multiply_subtract_fusion = (f32[1,2,256,1024]{2,3,0,1:T(8,128)}, f32[1,2,256,1024]{2,3,0,1:T(8,128)}) fusion(f32[3,2,256,1024]{2,3,0,1:T(8,128)} %get-tuple-element.306, f32[3,2,256,1024]{2,3,0,1:T(8,128)} %get-tuple-element.307), kind=kLoop, calls=%fused_computation.124 | loop fusion | flops 3145728 | bytes 16777216 | tf_op jit(solution)/shard_map/sub | solution.py:173
  377.7 56.3 %conditional.3 = (f32[3,1,256,1024]{3,1,0,2:T(1,128)}, f32[3,1,256,1024]{3,1,0,2:T(1,128)}) conditional(s32[]{:T(128)} %convert_element_type.132, (f32[3,2,256,1024]{2,3,0,1:T(8,128)S(1)}, f32[256,256]{1,0:T(8,128)S(1)}, f32[3,2,256,1024]{2,3,0,1:T(8,128)S(1)}, f32[256,256]{1,0:T(8,128)S(1)}, f32[256,256]{1,0:T(8,128)S(1)}, ...), branch_computations={%region_2.3_spmd, %region_3.4_spmd} | conditional | flops 14500233216 | bytes 165152912 | solution.py:111
  405.8 8.6 %copy.92 = f32[3,1,256,1024]{3,1,0,2:T(1,128)} copy(f32[3,1,256,1024]{2,3,0,1:T(8,128)} %subtract_bitcast_fusion.2) | data formatting | bytes 6291456 | tf_op jit(solution)/shard_map/cond | solution.py:111
  428.0 5.6 copy.94
  433.9 8.5 %maximum_bitcast_fusion = f32[3,2,1,256,1024]{4,1,0,2,3:T(2,128)S(1)} fusion(f32[3,1,256,1024]{3,1,0,2:T(1,128)} %get-tuple-element.309, f32[3,1,256,1024]{3,1,0,2:T(1,128)} %get-tuple-element.308), kind=kLoop, calls=%fused_computation.86 | loop fusion | flops 1572864 | bytes 12582912 | tf_op jit(solution)/shard_map/broadcast_in_dim | solution.py:112
  442.5 139.4 %all_to_all.45 = f32[3,2,1,256,1024]{4,1,0,2,3:T(2,128)S(1)} all-to-all(f32[3,2,1,256,1024]{4,1,0,2,3:T(2,128)S(1)} %maximum_bitcast_fusion), channel_id=1, replica_groups=mesh['ctx'=8,'ch'=4] {'ctx'}, dimensions={3} | all-to-all | bytes 12582912 | tf_op jit(solution)/shard_map/all_to_all | solution.py:113
  585.0 7.4 %fusion.85 = f32[3,32,1024,8]{2,3,1,0:T(8,128)S(1)} fusion(f32[3,1,8,32,1024]{4,3,2,1,0:T(8,128)S(1)} %get-tuple-element.326, f32[3,1,8,32,1024]{4,3,2,1,0:T(8,128)S(1)} %get-tuple-element.325, f32[8,32]{0,1:T(8,128)S(1)} %get-tuple-element.344, f32[8,32]{0,1:T(8,128)S(1)} %get-tuple-element.343, f32[8]{0:T(128)S(1)} %fusion.159, ...), kind=kOutput, calls=%fused_computation.111 | convolution fusion | flops 77857792 | bytes 9439272 | tf_op jit(solution)/shard_map/ak,skbc->sabc/dot_general | solution.py:22
  592.4 7.9 %multiply_bitcast_fusion = f32[3,8,32,1024]{3,1,2,0:T(8,128)S(1)} fusion(f32[3,32,1024,8]{2,3,1,0:T(8,128)S(1)} %fusion.85, f32[3,1,8,32,1024]{4,3,2,1,0:T(8,128)S(1)} %get-tuple-element.326, f32[3,1,8,32,1024]{4,3,2,1,0:T(8,128)S(1)} %get-tuple-element.325, f32[8,32]{0,1:T(8,128)S(1)} %get-tuple-element.344, f32[8,32]{0,1:T(8,128)S(1)} %get-tuple-element.343, ...), kind=kOutput, calls=%fused_computation.110 | convolution fusion | flops 79430656 | bytes 12584968 | tf_op jit(solution)/shard_map/ak,skbc->sabc/dot_general | solution.py:22
  602.1 73.8 %all_to_all.46 = f32[3,8,32,1024]{3,2,0,1:T(8,128)S(1)} all-to-all(f32[3,8,32,1024]{3,2,0,1:T(8,128)S(1)} %copy.81), channel_id=1, replica_groups=mesh['ctx'=8,'ch'=4] {'ctx'}, dimensions={1} | all-to-all | bytes 6291456 | tf_op jit(solution)/shard_map/all_to_all | solution.py:182
  688.1 35.7 %all-reduce.2 = (f32[3,3,1024]{2,0,1:T(4,128)S(1)}, f32[1024]{0:T(1024)}) all-reduce(f32[3,3,1024]{2,0,1:T(4,128)S(1)} %pad_maximum_fusion.7, f32[1024]{0:T(1024)S(1)} %get-tuple-element.332), channel_id=1, replica_groups=mesh['ctx'=8,'ch'=4] {'ctx'}, use_global_device_ids=true, to_apply=%region_7.8 | all-reduce | flops 10240 | bytes 81920 | tf_op jit(solution)/shard_map/psum | solution.py:204
  (119 shorter events, 95.7 us)
Async XLA Ops:
  7.2 7.8 %copy-start.23 = (bf16[256,1024]{1,0:T(8,128)(2,1)S(1)}, bf16[256,1024]{1,0:T(8,128)(2,1)}, u32[]{:S(2)}) copy-start(bf16[256,1024]{1,0:T(8,128)(2,1)} %param.14) | copy-start | bytes 1572868
  7.2 7.8 %copy-start.24 = (bf16[256,1024]{1,0:T(8,128)(2,1)S(1)}, bf16[256,1024]{1,0:T(8,128)(2,1)}, u32[]{:S(2)}) copy-start(bf16[256,1024]{1,0:T(8,128)(2,1)} %param.13) | copy-start | bytes 1572868
  7.2 7.8 %copy-start.25 = (bf16[256,1024]{1,0:T(8,128)(2,1)S(1)}, bf16[256,1024]{1,0:T(8,128)(2,1)}, u32[]{:S(2)}) copy-start(bf16[256,1024]{1,0:T(8,128)(2,1)} %param.12) | copy-start | bytes 1572868
  7.2 39.6 %all-gather.2.cloned.1.call-start = ((), (), s32[]{:S(2)}) async-start(), calls=%async_computation.4 | async-start | bytes 5242880 | tf_op jit(solution)/shard_map/all_gather | solution.py:155
  8.7 6.3 collective-permute-start
  17.1 42.0 %copy-start.15 = (f32[3,256,1024]{2,1,0:T(8,128)}, f32[3,256,1024]{2,1,0:T(8,128)S(1)}, u32[]{:S(2)}) copy-start(f32[3,256,1024]{2,1,0:T(8,128)S(1)} %multiply_add_fusion) | copy-start | bytes 9437188
  66.1 76.6 %all-to-all-start = ((f32[3,1,256,1024]{3,1,0,2:T(1,128)}), f32[3,1,256,1024]{3,1,0,2:T(1,128)S(1)}, u32[]{:S(2)}, u32[]{:S(2)}) async-start(f32[3,1,256,1024]{3,1,0,2:T(1,128)} %copy.66), calls=%async_computation | async-start | bytes 6291456 | tf_op jit(solution)/shard_map/all_to_all | solution.py:163
  163.0 142.5 %all-to-all-start.1 = ((f32[3,2,8,32,1024]{4,3,0,1,2:T(8,128)}), f32[3,2,8,32,1024]{4,3,0,1,2:T(8,128)}, u32[]{:S(2)}, u32[]{:S(2)}) async-start(f32[3,2,8,32,1024]{4,3,0,1,2:T(8,128)} %copy.70), calls=%async_computation.1 | async-start | bytes 12582912 | tf_op jit(solution)/shard_map/all_to_all | solution.py:61
  168.9 141.1 %copy-start.11 = (f32[256,256]{1,0:T(8,128)}, f32[256,256]{1,0:T(8,128)S(1)}, u32[]{:S(2)}) copy-start(f32[256,256]{1,0:T(8,128)S(1)} %get-tuple-element.347) | copy-start | bytes 786436
  332.7 2.9 copy-start.3
  358.2 7.9 %copy-start.8 = (f32[3,2,256,1024]{2,3,0,1:T(8,128)S(1)}, f32[3,2,256,1024]{2,3,0,1:T(8,128)}, u32[]{:S(2)}) copy-start(f32[3,2,256,1024]{2,3,0,1:T(8,128)} %get-tuple-element.307) | copy-start | bytes 18874372
  358.2 9.8 %copy-start.9 = (f32[3,2,256,1024]{2,3,0,1:T(8,128)S(1)}, f32[3,2,256,1024]{2,3,0,1:T(8,128)}, u32[]{:S(2)}) copy-start(f32[3,2,256,1024]{2,3,0,1:T(8,128)} %get-tuple-element.306) | copy-start | bytes 18874372
  372.0 3.8 copy-start.18
  372.0 4.1 copy-start.19
  372.0 4.7 copy-start.20
  396.7 2.9 copy-start.4
  396.7 4.6 copy-start.6
  414.4 4.8 copy-start.5
  419.1 2.8 copy-start.7
  679.4 6.5 copy-start.1
  679.4 6.5 copy-start.28
  679.5 6.5 copy-start.30
  679.5 6.5 copy-start.32
  679.5 6.0 collective-permute-start.1
  (14 other events, 28.0 us)
Sparse Core Ops, SparseCore 0:
  9.6 37.1 all-gather.1
where the time goes:
time: 741 us; the launch traced here: 733 us
  blocking collectives  249 us (34%)
  waiting for transfers between devices  241 us (33%)
  matrix products  88.5 us (12%)
  local copies, waits for them, and re-layouts  51.7 us (7%)
  other arithmetic  41.7 us (6%)
  loops' own time  29 us (4%)
  starting transfers between devices  16.9 us (2%)
  between operations  14.7 us (2%)
    all_to_all x1, blocking collectives, inverse_half(): lax.all_to_all(sending, 'ctx', split_axis=3, concat_axis=2, tiled=True)  139 us
    all_to_all x1, waiting for transfers between devices, forward_half(): lax.all_to_all(jnp.stack([second_real, second_imag], axis=1), 'ctx', spli...  137 us
    dot_general x18, matrix products, mat_apply(): return jnp.einsum(form, table, data, precision=lax.Precision.HIGHEST)  76.2 us
    all_to_all x1, blocking collectives, per_device(): lax.all_to_all(fields, 'ctx', split_axis=1, concat_axis=2, tiled=True)  73.8 us
    all_to_all x1, waiting for transfers between devices, per_device(): lax.all_to_all(signals[:, None], 'ctx', split_axis=2, concat_axis=1, tile...  70.8 us
    psum x1, blocking collectives, per_device(): d_short, d_skip = lax.psum((short_terms, skip_term), 'ctx')  35.7 us
    all_gather x1, waiting for transfers between devices, per_device(): lax.all_gather(d_out, 'ch', axis=1, tiled=True)  28.4 us
    another operation x1, loops' own time, inverse_half(): lax.cond(position == 0, corner_back, plain_back, (spec_real, spec_imag))  19.4 us
  transfers between devices with their start and end apart: 5, of which 5 were waited for; matrix products, arithmetic and copies ran while one was open for 1% of the time, Pallas kernels for 0%

commit v1 on v0

v1 whole, which is shorter than its diff:
```python
import functools
import math

import jax
import jax.numpy as jnp
import numpy as np
from jax import lax
from jax.experimental import pallas as pl
from jax.experimental.pallas import tpu as pltpu
from jax.sharding import PartitionSpec as P

PAD = 8
TAIL = 16
PARAMS = dict(vmem_limit_bytes=60 * 1024 * 1024)
F32 = jnp.float32
BF16 = jnp.bfloat16


def split_table(table):
    table = table.astype(np.float32)
    high = table.astype(BF16)
    low = (table - high.astype(np.float32)).astype(BF16)
    return np.concatenate([high[None], low[None]], axis=0)


def tables(block):
    freq = np.arange(block)[:, None]
    place = np.arange(block)[None, :]
    angle = (2 * freq + 1) * place % (4 * block) * (math.pi / (2 * block))
    forward = np.concatenate([np.cos(angle), -np.sin(angle)], axis=0)
    return split_table(forward), split_table(forward.T / block)


def shifted(block, axis, distance):
    devices = range(lax.axis_size(axis))
    route = [(i - distance, i) for i in devices if i - distance in devices]
    return lax.ppermute(block, axis, route)


def fill(scratch, before, own, after, rim):
    rows = own.shape[0]
    scratch[0:PAD, :] = jnp.zeros_like(scratch[0:PAD, :])
    scratch[PAD + rows :, :] = jnp.zeros_like(scratch[PAD + rows :, :])
    scratch[PAD - rim : PAD, :] = before.astype(F32)
    scratch[PAD : PAD + rows, :] = own.astype(F32)
    if after is not None:
        scratch[PAD + rows : PAD + rows + rim, :] = after.astype(F32)


def short(scratch, taps, rows, lanes, s):
    total = None
    for j in range(taps.shape[1]):
        term = taps[s, j : j + 1, lanes] * scratch[PAD - j : PAD - j + rows, :]
        total = term if total is None else total + term
    return total


def enter_kernel(pieces, k_ref, v_ref, before, long_ref, taps, mh_ref, ext):
    rows, width = k_ref.shape
    cw = width // pieces
    rim = before.shape[1]
    for c in range(pieces):
        lanes = slice(c * cw, (c + 1) * cw)
        fill(ext, before[1, :, lanes], k_ref[:, lanes], None, rim)
        keyed = short(ext, taps, rows, lanes, 1)
        fill(ext, before[2, :, lanes], v_ref[:, lanes], None, rim)
        mh_ref[c, 0] = (keyed * short(ext, taps, rows, lanes, 2)).astype(BF16)
        mh_ref[c, 1] = long_ref[:, lanes].astype(BF16)


def grad_kernel(pieces, q_ref, before, go_ref, taps, g_ref, ext):
    rows, width = q_ref.shape
    cw = width // pieces
    rim = before.shape[1]
    for c in range(pieces):
        lanes = slice(c * cw, (c + 1) * cw)
        fill(ext, before[0, :, lanes], q_ref[:, lanes], None, rim)
        g_ref[c] = (go_ref[:, lanes].astype(F32) * short(ext, taps, rows, lanes, 0)).astype(BF16)


def times(a, b):
    return a[0] * b[0] - a[1] * b[1], a[0] * b[1] + a[1] * b[0]


def conj_times(a, b):
    return a[0] * b[0] + a[1] * b[1], a[0] * b[1] - a[1] * b[0]


def add(a, b):
    return b if a is None else (a[0] + b[0], a[1] + b[1])


def spectra(table, blocks, spec):
    for at in range(0, len(blocks), 2):
        pair = blocks[at : at + 2]
        data = jnp.concatenate([ref[...] for ref, _, _ in pair], axis=1)
        out = jnp.dot(table[0], data, preferred_element_type=F32) + jnp.dot(
            table[1], data, preferred_element_type=F32
        )
        cw = data.shape[1] // len(pair)
        for p, (_, s, i) in enumerate(pair):
            spec[s, i] = out[:, p * cw : (p + 1) * cw]


def mix_spectra(spec, primed, held):
    count, rows2, cw = spec.shape[1:]
    half = rows2 // 2
    step = 8
    sign = 1.0 - 2.0 * (lax.broadcasted_iota(jnp.int32, (step, cw), 0) % 2).astype(F32)

    def primes(blocks):
        out = [blocks[0]]
        for d in range(1, count):
            re, im = blocks[d]
            old_re, old_im = blocks[d - 1]
            out.append((re - sign * old_im, im + sign * old_re))
        return out

    def chunk(r, carry):
        low = pl.ds(pl.multiple_of(r * step, step), step)
        high = pl.ds(pl.multiple_of(half + r * step, step), step)

        def load(s, i):
            return spec[s, i, low, :], spec[s, i, high, :]

        def save(s, i, value):
            spec[s, i, low, :] = value[0]
            spec[s, i, high, :] = value[1]

        if count <= 8:
            mixed = [load(0, i) for i in range(count)]
            taps = primes([load(1, i) for i in range(count)])
            for i in range(count):
                total = None
                for d in range(i + 1):
                    total = add(total, times(taps[d], mixed[i - d]))
                save(0, i, total)
            grads = [load(2, i) for i in range(count)]
            for b in range(count):
                total = None
                for e in range(count - b):
                    total = add(total, conj_times(taps[e], grads[b + e]))
                save(1, b, total)
            mixed = primes(mixed)
            for b in range(count):
                total = None
                for e in range(count - b):
                    total = add(total, conj_times(mixed[e], grads[b + e]))
                save(2, b, total)
            return carry

        for s in range(2):
            for d, value in enumerate(primes([load(s, i) for i in range(count)])):
                primed[s, d, 0] = value[0]
                primed[s, d, 1] = value[1]
        zero = jnp.zeros((step, cw), F32)

        def one(b, inner):
            def of_y(d, total):
                return add(total, times((primed[1, d, 0], primed[1, d, 1]), load(0, b - d)))

            def of_g(e, totals):
                grad = load(2, b + e)
                first = conj_times((primed[1, e, 0], primed[1, e, 1]), grad)
                second = conj_times((primed[0, e, 0], primed[0, e, 1]), grad)
                return add(totals[0], first), add(totals[1], second)

            held[0, b, 0], held[0, b, 1] = lax.fori_loop(0, b + 1, of_y, (zero, zero))
            first, second = lax.fori_loop(0, count - b, of_g, ((zero, zero), (zero, zero)))
            held[1, b, 0], held[1, b, 1] = first
            held[2, b, 0], held[2, b, 1] = second
            return inner

        lax.fori_loop(0, count, one, 0)
        for s in range(3):
            for b in range(count):
                save(s, b, (held[s, b, 0], held[s, b, 1]))
        return carry

    lax.fori_loop(0, half // step, chunk, 0)


def back_pair(table, values):
    data = jnp.concatenate(values, axis=1)
    high = data.astype(BF16)
    low = (data - high.astype(F32)).astype(BF16)
    out = (
        jnp.dot(table[0], high, preferred_element_type=F32)
        + jnp.dot(table[0], low, preferred_element_type=F32)
        + jnp.dot(table[1], high, preferred_element_type=F32)
    )
    cw = data.shape[1] // len(values)
    return [out[:, p * cw : (p + 1) * cw].astype(BF16) for p in range(len(values))]


def conv_kernel(mh_ref, g_ref, forward, inverse, out_ref, spec, primed, held):
    count, _, rows, cw = mh_ref.shape
    blocks = []
    for i in range(count):
        blocks += [(mh_ref.at[i, 0], 0, i), (mh_ref.at[i, 1], 1, i)]
    blocks += [(g_ref.at[i], 2, i) for i in range(count)]
    spectra(forward, blocks, spec)
    mix_spectra(spec, primed, held)
    base = (0, rows + TAIL, 2 * (rows + TAIL))
    for s in range(3):
        at = base[s]
        for i in range(0, count, 2):
            many = min(2, count - i)
            results = back_pair(inverse, [spec[s, i + p] for p in range(many)])
            for p, value in enumerate(results):
                out_ref[i + p, at : at + rows, :] = value
                if s < 2 and i + p > 0:
                    out_ref[i + p - 1, at + rows : at + rows + TAIL, :] = value[:TAIL]
        if s < 2:
            out_ref[count - 1, at + rows : at + rows + TAIL, :] = jnp.zeros((TAIL, cw), BF16)


def leave_kernel(pieces, q_ref, k_ref, v_ref, before, after, go_ref, go_after, taps, skip_ref,
                 got_ref, dq_ref, dk_ref, dv_ref, long_ref, sums_ref, ext, go_ext, grad_ext):
    rows, width = q_ref.shape
    cw = width // pieces
    rim = before.shape[1]
    tap_count = taps.shape[1]
    more = rows + PAD
    sums_ref[...] = jnp.zeros_like(sums_ref)
    for c in range(pieces):
        lanes = slice(c * cw, (c + 1) * cw)
        filtered = []
        for s, ref in enumerate((q_ref, k_ref, v_ref)):
            fill(ext.at[s], before[s, :, lanes], ref[:, lanes], after[s, :, lanes], rim)
            filtered.append(short(ext.at[s], taps, more, lanes, s))
        fill(go_ext, jnp.zeros((rim, cw), F32), go_ref[:, lanes], go_after[:, lanes], rim)
        grad_o = go_ext[PAD : PAD + more, :]
        mixed = filtered[1] * filtered[2]
        grad_y = grad_o * filtered[0]
        gain = skip_ref[:, lanes]
        y_full = got_ref[c, 0:more, :].astype(F32) + gain * mixed
        at = rows + TAIL
        grad_mixed = got_ref[c, at : at + more, :].astype(F32) + gain * grad_y
        grad_ext[0, 0:more, :] = grad_o * y_full
        grad_ext[1, 0:more, :] = grad_mixed * filtered[2]
        grad_ext[2, 0:more, :] = grad_mixed * filtered[1]
        long_ref[:, lanes] = got_ref[c, 2 * at : 2 * at + rows, :].astype(F32)
        for s, ref in enumerate((dq_ref, dk_ref, dv_ref)):
            total = None
            own = grad_ext[s, 0:rows, :]
            for j in range(tap_count):
                term = taps[s, j : j + 1, lanes] * grad_ext[s, j : j + rows, :]
                total = term if total is None else total + term
                stream = ext[s, PAD - j : PAD - j + rows, :]
                row = s * tap_count + j
                sums_ref[row : row + 1, lanes] = jnp.sum(own * stream, axis=0, keepdims=True)
            ref[:, lanes] = total.astype(BF16)
        row = 3 * tap_count
        sums_ref[row : row + 1, lanes] = jnp.sum(
            grad_y[0:rows] * mixed[0:rows], axis=0, keepdims=True
        )


def call(kernel, out_shape, scratch, *args, **params):
    return pl.pallas_call(
        kernel,
        out_shape=out_shape,
        in_specs=[pl.BlockSpec(memory_space=pltpu.VMEM)] * len(args),
        out_specs=jax.tree.map(lambda _: pl.BlockSpec(memory_space=pltpu.VMEM), out_shape),
        scratch_shapes=scratch,
        compiler_params=pltpu.CompilerParams(**PARAMS, **params),
    )(*args)


def per_device(queries, keys, values, long_filter, short_filters, skip, w_out, d_out):
    ctx = lax.axis_size("ctx")
    rows, width = queries.shape
    cw = width // ctx
    tap_count = short_filters.shape[1]
    rim = tap_count - 1
    ends = jnp.stack([queries[rows - rim :], keys[rows - rim :], values[rows - rim :]])
    starts = jnp.stack([queries[:rim], keys[:rim], values[:rim]])
    before = shifted(ends, "ctx", 1)
    after = shifted(starts, "ctx", -1)
    ext = pltpu.VMEM((rows + 4 * PAD, cw), F32)
    shape = jax.ShapeDtypeStruct
    mh = call(
        functools.partial(enter_kernel, ctx),
        shape((ctx, 2, rows, cw), BF16), [ext],
        keys, values, before, long_filter, short_filters,
    )
    mh = lax.all_to_all(mh, "ctx", split_axis=0, concat_axis=0, tiled=True)
    grad_o = lax.dot_general(
        lax.all_gather(d_out, "ch", axis=1, tiled=True),
        w_out,
        (((1,), (1,)), ((), ())),
        preferred_element_type=F32,
    ).astype(BF16)
    go_after = shifted(grad_o[:rim], "ctx", -1)
    g = call(
        functools.partial(grad_kernel, ctx),
        shape((ctx, rows, cw), BF16), [ext],
        queries, before, grad_o, short_filters,
    )
    g = lax.all_to_all(g, "ctx", split_axis=0, concat_axis=0, tiled=True)
    forward, inverse = tables(rows)
    spare = ctx if ctx > 8 else 1
    back = call(
        conv_kernel,
        shape((ctx, 3 * rows + 2 * TAIL, cw), BF16),
        [pltpu.VMEM((3, ctx, 2 * rows, cw), F32), pltpu.VMEM((2, spare, 2, 8, cw), F32),
         pltpu.VMEM((3, spare, 2, 8, cw), F32)],
        mh, g, jnp.asarray(forward), jnp.asarray(inverse),
    )
    back = lax.all_to_all(back, "ctx", split_axis=0, concat_axis=0, tiled=True)
    stream = shape((rows, width), BF16)
    dq, dk, dv, d_long, sums = call(
        functools.partial(leave_kernel, ctx),
        (stream, stream, stream, shape((rows, width), F32), shape((16, width), F32)),
        [pltpu.VMEM((3, rows + 4 * PAD, cw), F32), ext, pltpu.VMEM((3, rows + 4 * PAD, cw), F32)],
        queries, keys, values, before, after, grad_o, go_after, short_filters, skip[None], back,
    )
    sums = lax.psum(sums, "ctx")
    d_short = sums[: 3 * tap_count].reshape(3, tap_count, width)
    return dq, dk, dv, d_long, d_short, sums[3 * tap_count]


def solution(mesh):
    in_specs = (
        P("ctx", "ch"),
        P("ctx", "ch"),
        P("ctx", "ch"),
        P("ctx", "ch"),
        P(None, None, "ch"),
        P("ch"),
        P("ch", None),
        P("ctx", "ch"),
    )
    out_specs = (
        P("ctx", "ch"),
        P("ctx", "ch"),
        P("ctx", "ch"),
        P("ctx", "ch"),
        P(None, None, "ch"),
        P("ch"),
    )
    return jax.shard_map(
        per_device, mesh=mesh, in_specs=in_specs, out_specs=out_specs, check_vma=False
    )
```

time: 741 us -> 222 us (0.30)
  blocking collectives: 249 us -> 20.5 us
  waiting for transfers between devices: 241 us -> 125 us
  matrix products: 88.5 us -> 12.4 us
  local copies, waits for them, and re-layouts: 51.7 us -> 6.9 us
  other arithmetic: 41.7 us -> 0.05 us
  loops' own time: 29 us -> 0 us
  Pallas kernels: 0 us -> 24.3 us
    all_to_all x2 -> x1, blocking collectives: 213 us -> 20.5 us  [per_device(): g = lax.all_to_all(g, 'ctx', split_axis=0, concat_axis=0, tiled=True)]
    all_to_all x2, waiting for transfers between devices: 207 us -> 29.7 us  [the longest x1 29.7 us: per_device(): back = lax.all_to_all(back, 'ctx', split_axis=0, concat_axis=0, tiled=True)]
    dot_general x18 -> x0, matrix products: 76.2 us -> none  [mat_apply(): return jnp.einsum(form, table, data, precision=lax.Precision.HIGHEST)]
    psum x0 -> x1, waiting for transfers between devices: none -> 67.4 us  [per_device(): sums = lax.psum(sums, 'ctx')]
    psum x1 -> x0, blocking collectives: 35.7 us -> none  [per_device(): d_short, d_skip = lax.psum((short_terms, skip_term), 'ctx')]
    another operation x2 -> x0, loops' own time: 29 us -> none  [the longest x1 19.4 us: inverse_half(): lax.cond(position == 0, corner_back, plain_back, (spec_real, spec_imag))]
    pallas_call x0 -> x4, Pallas kernels: none -> 24.3 us  [call(): pl.pallas_call(kernel, out_shape=out_shape, in_specs=[pl.BlockSpec(memory...]
    cond x20 -> x0, local copies, waits for them, and re-layouts: 18.6 us -> none  [the longest x2 14.2 us: inverse_half(): lax.cond(position == 0, corner_back, plain_back, (spec_real, spec_imag))]
  transfers between devices with their start and end apart: 5 -> 7, of which waited for: 5 -> 6; matrix products, arithmetic and copies ran while one was open for 1% -> 7% of each run, Pallas kernels for 0% -> 3%
where the time goes in v1:
time: 222 us; the launch traced here: 221 us
  waiting for transfers between devices  125 us (56%)
  Pallas kernels  24.3 us (11%)
  blocking collectives  20.5 us (9%)
  starting transfers between devices  18.2 us (8%)
  between operations  14.1 us (6%)
  matrix products  12.4 us (6%)
  local copies, waits for them, and re-layouts  6.9 us (3%)
    psum x1, waiting for transfers between devices, per_device(): sums = lax.psum(sums, 'ctx')  67.4 us
    all_to_all x1, waiting for transfers between devices, per_device(): back = lax.all_to_all(back, 'ctx', split_axis=0, concat_axis=0, tiled=True)  29.7 us
    pallas_call x4, Pallas kernels, call(): pl.pallas_call(kernel, out_shape=out_shape, in_specs=[pl.BlockSpec(memory...  24.3 us
    all_to_all x1, blocking collectives, per_device(): g = lax.all_to_all(g, 'ctx', split_axis=0, concat_axis=0, tiled=True)  20.5 us
    all_gather x1, waiting for transfers between devices, per_device(): lax.all_gather(d_out, 'ch', axis=1, tiled=True)  20.3 us
    dot_general x1, matrix products, per_device(): lax.dot_general(lax.all_gather(d_out, 'ch', axis=1, tiled=True), w_out, (...  12.4 us
    ppermute x3, starting transfers between devices, shifted(): return lax.ppermute(block, axis, route)  7.65 us
    all_to_all x1, starting transfers between devices, per_device(): mh = lax.all_to_all(mh, 'ctx', split_axis=0, concat_axis=0, tiled=True)  6.8 us
  transfers between devices with their start and end apart: 7, of which 6 were waited for; matrix products, arithmetic and copies ran while one was open for 7% of the time, Pallas kernels for 3%

profile of v1, /device:TPU:0, one launch (start us, length us, event | category | flops | bytes accessed | tf_op | source)
XLA Modules:
  0.0 221.1 jit_solution(2433860884389762679)
XLA Ops:
  7.2 0.7 all-gather.2.cloned.1.call-update
  7.9 0.7 slice_bitcast_fusion.2
  8.7 0.8 slice_bitcast_fusion
  9.5 4.9 %collective-permute-start = (bf16[3,2,1024]{2,1,0:T(2,128)(2,1)S(1)}, bf16[3,2,1024]{2,1,0:T(2,128)(2,1)S(1)}, u32[]{:S(2)}, u32[]{:S(2)}) collective-permute-start(bf16[3,2,1024]{2,1,0:T(2,128)(2,1)S(1)} %pad_maximum_fusion), channel_id=1, source_target_pairs={{0,4},{4,8},{8,12},{12,16},{16,20},{20,24},{24,28},{1,5},{5,9},{9,... | collective-permute-start | bytes 36872 | tf_op jit(solution)/shard_map/ppermute | solution.py:37
  14.4 1.4 collective-permute-done.before
  15.8 0.6 copy-done.2
  16.4 3.3 %shard_map.145 = bf16[8,2,256,128]{3,2,1,0:T(8,128)(2,1)} custom-call(bf16[256,1024]{1,0:T(8,128)(2,1)} %k_ref.3, bf16[256,1024]{1,0:T(8,128)(2,1)} %v_ref.3, bf16[3,2,1024]{2,1,0:T(2,128)(2,1)} %copy-done.2, f32[256,1024]{1,0:T(8,128)} %long_ref.1, f32[3,3,1024]{2,1,0:T(4,128)} %taps.5), custom_call_target="tpu_custom_call" | custom-call | tf_op jit(solution)/shard_map/pallas_call | solution.py:261
  19.6 6.8 %all-to-all-start = ((bf16[8,2,256,128]{3,2,1,0:T(8,128)(2,1)}), bf16[8,2,256,128]{3,2,1,0:T(8,128)(2,1)S(1)}, u32[]{:S(2)}, u32[]{:S(2)}) async-start(bf16[8,2,256,128]{3,2,1,0:T(8,128)(2,1)} %shard_map.145), calls=%async_computation | async-start | bytes 2097152 | tf_op jit(solution)/shard_map/all_to_all | solution.py:288
  26.4 20.3 %all-gather.2.cloned.1.call-done = bf16[256,8192]{1,0:T(8,128)(2,1)} async-done(((bf16[256,2048]{1,0:T(8,128)(2,1)}), bf16[256,8192]{1,0:T(8,128)(2,1)}) %all-gather.2.cloned.1.call-update) | async-done | bytes 4194320 | tf_op jit(solution)/shard_map/all_gather | solution.py:290
  46.7 12.4 %convolution_convert_fusion.go_ref = bf16[256,1024]{1,0:T(8,128)(2,1)} fusion(bf16[256,8192]{1,0:T(8,128)(2,1)} %all-gather.2.cloned.1.call-done, bf16[1024,8192]{1,0:T(8,128)(2,1)} %param.16), kind=kOutput, calls=%fused_computation | convolution fusion | flops 4295229440 | bytes 21495808 | tf_op jit(solution)/shard_map/dot_general | solution.py:289
  59.1 2.5 %shard_map.146 = bf16[8,256,128]{2,1,0:T(8,128)(2,1)} custom-call(bf16[256,1024]{1,0:T(8,128)(2,1)} %q_ref.3, bf16[3,2,1024]{2,1,0:T(2,128)(2,1)} %copy-done.2, bf16[256,1024]{1,0:T(8,128)(2,1)} %convolution_convert_fusion.go_ref, f32[3,3,1024]{2,1,0:T(4,128)} %taps.5), custom_call_target="tpu_custom_call" | custom-call | tf_op jit(solution)/shard_map/pallas_call | solution.py:261
  61.6 20.5 %all_to_all.15.g_ref = bf16[8,256,128]{2,1,0:T(8,128)(2,1)} all-to-all(bf16[8,256,128]{2,1,0:T(8,128)(2,1)} %shard_map.146), channel_id=1, replica_groups=mesh['ctx'=8,'ch'=4] {'ctx'}, dimensions={0} | all-to-all | bytes 1048576 | tf_op jit(solution)/shard_map/all_to_all | solution.py:301
  82.1 11.2 %shard_map.147 = bf16[8,800,128]{2,1,0:T(8,128)(2,1)} custom-call(bf16[8,2,256,128]{3,2,1,0:T(8,128)(2,1)} %copy-done.1, bf16[8,256,128]{2,1,0:T(8,128)(2,1)} %all_to_all.15.g_ref, bf16[2,512,256]{2,1,0:T(8,128)(2,1)} %constant.4.clone.forward, bf16[2,256,512]{2,1,0:T(8,128)(2,1)} %constant.5.clone.inverse), custom_call_target="tpu_custom_call" | custom-call | tf_op jit(solution)/shard_map/pallas_call | solution.py:261
  93.3 3.6 %all-to-all-start.2 = ((bf16[8,800,128]{2,1,0:T(8,128)(2,1)}), bf16[8,800,128]{2,1,0:T(8,128)(2,1)S(1)}, u32[]{:S(2)}, u32[]{:S(2)}) async-start(bf16[8,800,128]{2,1,0:T(8,128)(2,1)} %shard_map.147), calls=%async_computation.2 | async-start | bytes 3276800 | tf_op jit(solution)/shard_map/all_to_all | solution.py:311
  97.0 1.3 collective-permute-start.1
  98.3 0.7 slice.36
  99.0 1.5 collective-permute-start.2
  100.5 5.1 %collective-permute-done.1.after = bf16[3,2,1024]{2,1,0:T(2,128)(2,1)S(1)} collective-permute-done((bf16[3,2,1024]{2,1,0:T(2,128)(2,1)S(1)}, bf16[3,2,1024]{2,1,0:T(2,128)(2,1)S(1)}, u32[]{:S(2)}, u32[]{:S(2)}) %collective-permute-start.1) | collective-permute-done | bytes 12320 | tf_op jit(solution)/shard_map/ppermute | solution.py:37
  105.8 29.7 %all-to-all-done.2.got_ref = bf16[8,800,128]{2,1,0:T(8,128)(2,1)S(1)} async-done(((bf16[8,800,128]{2,1,0:T(8,128)(2,1)}), bf16[8,800,128]{2,1,0:T(8,128)(2,1)S(1)}, u32[]{:S(2)}, u32[]{:S(2)}) %all-to-all-start.2) | async-done | bytes 1638432 | tf_op jit(solution)/shard_map/all_to_all | solution.py:311
  135.5 1.2 copy-done
  136.7 7.4 %shard_map.148 = (bf16[256,1024]{1,0:T(8,128)(2,1)}, bf16[256,1024]{1,0:T(8,128)(2,1)}, bf16[256,1024]{1,0:T(8,128)(2,1)}, f32[256,1024]{1,0:T(8,128)}, f32[16,1024]{1,0:T(8,128)}) custom-call(bf16[256,1024]{1,0:T(8,128)(2,1)} %q_ref.3, bf16[256,1024]{1,0:T(8,128)(2,1)} %k_ref.3, bf16[256,1024]{1,0:T(8,128)(2,1)} %v_ref.3, bf16[3,2,1024]{2,1,0:T(2,128)(2,1)} %copy-done.2, ...), custom_call_target="tpu_custom_call" | custom-call | tf_op jit(solution)/shard_map/pallas_call | solution.py:261
  144.0 67.4 %all-reduce.2.cloned.1.call-done = f32[16,1024]{1,0:T(8,128)} async-done(((f32[16,1024]{1,0:T(8,128)}), f32[16,1024]{1,0:T(8,128)}) %all-reduce.2.cloned.1.call-update) | async-done | bytes 65552 | tf_op jit(solution)/shard_map/psum | solution.py:319
  211.4 1.5 reshape.15
  212.9 1.4 slice.38
  (15 shorter events, 0.3 us)
Async XLA Ops:
  7.2 39.6 %all-gather.2.cloned.1.call-start = ((), (), s32[]{:S(2)}) async-start(), calls=%async_computation.3 | async-start | bytes 5242880 | tf_op jit(solution)/shard_map/all_gather | solution.py:290
  9.5 6.3 %collective-permute-start = (bf16[3,2,1024]{2,1,0:T(2,128)(2,1)S(1)}, bf16[3,2,1024]{2,1,0:T(2,128)(2,1)S(1)}, u32[]{:S(2)}, u32[]{:S(2)}) collective-permute-start(bf16[3,2,1024]{2,1,0:T(2,128)(2,1)S(1)} %pad_maximum_fusion), channel_id=1, source_target_pairs={{0,4},{4,8},{8,12},{12,16},{16,20},{20,24},{24,28},{1,5},{5,9},{9,... | collective-permute-start | bytes 36872 | tf_op jit(solution)/shard_map/ppermute | solution.py:37
  15.8 0.6 copy-start.2
  19.6 41.9 %all-to-all-start = ((bf16[8,2,256,128]{3,2,1,0:T(8,128)(2,1)}), bf16[8,2,256,128]{3,2,1,0:T(8,128)(2,1)S(1)}, u32[]{:S(2)}, u32[]{:S(2)}) async-start(bf16[8,2,256,128]{3,2,1,0:T(8,128)(2,1)} %shard_map.145), calls=%async_computation | async-start | bytes 2097152 | tf_op jit(solution)/shard_map/all_to_all | solution.py:288
  61.6 20.5 %copy-start.1 = (bf16[8,2,256,128]{3,2,1,0:T(8,128)(2,1)}, bf16[8,2,256,128]{3,2,1,0:T(8,128)(2,1)S(1)}, u32[]{:S(2)}) copy-start(bf16[8,2,256,128]{3,2,1,0:T(8,128)(2,1)S(1)} %all-to-all-done.mh_ref) | copy-start | bytes 3145732
  93.3 42.2 %all-to-all-start.2 = ((bf16[8,800,128]{2,1,0:T(8,128)(2,1)}), bf16[8,800,128]{2,1,0:T(8,128)(2,1)S(1)}, u32[]{:S(2)}, u32[]{:S(2)}) async-start(bf16[8,800,128]{2,1,0:T(8,128)(2,1)} %shard_map.147), calls=%async_computation.2 | async-start | bytes 3276800 | tf_op jit(solution)/shard_map/all_to_all | solution.py:311
  96.9 114.5 %all-reduce.2.cloned.1.call-start = ((), (), s32[]{:S(2)}) async-start(), calls=%async_computation.4 | async-start | bytes 131072 | tf_op jit(solution)/shard_map/psum | solution.py:319
  97.0 8.6 %collective-permute-start.1 = (bf16[3,2,1024]{2,1,0:T(2,128)(2,1)S(1)}, bf16[3,2,1024]{2,1,0:T(2,128)(2,1)S(1)}, u32[]{:S(2)}, u32[]{:S(2)}) collective-permute-start(bf16[3,2,1024]{2,1,0:T(2,128)(2,1)S(1)} %pad_maximum_fusion.1), channel_id=1, source_target_pairs={{4,0},{8,4},{12,8},{16,12},{20,16},{24,20},{28,24},{5,1},{9,5},{13... | collective-permute-start | bytes 36872 | tf_op jit(solution)/shard_map/ppermute | solution.py:37
  99.0 6.7 %collective-permute-start.2 = (bf16[2,1024]{1,0:T(2,128)(2,1)S(1)}, bf16[2,1024]{1,0:T(2,128)(2,1)S(1)}, u32[]{:S(2)}, u32[]{:S(2)}) collective-permute-start(bf16[2,1024]{1,0:T(2,128)(2,1)S(1)} %slice.36), channel_id=1, source_target_pairs={{4,0},{8,4},{12,8},{16,12},{20,16},{24,20},{28,24},{5,1},{9,5},{13... | collective-permute-start | bytes 12296 | tf_op jit(solution)/shard_map/ppermute | solution.py:37
  105.6 29.9 %copy-start.3 = (bf16[3,2,1024]{2,1,0:T(2,128)(2,1)}, bf16[3,2,1024]{2,1,0:T(2,128)(2,1)S(1)}, u32[]{:S(2)}) copy-start(bf16[3,2,1024]{2,1,0:T(2,128)(2,1)S(1)} %collective-permute-done.1.after) | copy-start | bytes 36868
  105.7 29.7 %copy-start.4 = (bf16[2,1024]{1,0:T(2,128)(2,1)}, bf16[2,1024]{1,0:T(2,128)(2,1)S(1)}, u32[]{:S(2)}) copy-start(bf16[2,1024]{1,0:T(2,128)(2,1)S(1)} %collective-permute-done.2.go_after) | copy-start | bytes 12292
  135.5 1.2 copy-start
Sparse Core Ops, SparseCore 0:
  9.5 37.1 all-gather.1
  144.2 67.1 all-reduce.1

commit v2 on v1

--- a/solution.py
+++ b/solution.py
@@ -14,6 +14,7 @@
 PARAMS = dict(vmem_limit_bytes=60 * 1024 * 1024)
 F32 = jnp.float32
 BF16 = jnp.bfloat16
+MESH = pl.DeviceIdType.MESH
 
 
 def split_table(table):
@@ -68,16 +69,6 @@
         mh_ref[c, 1] = long_ref[:, lanes].astype(BF16)
 
 
-def grad_kernel(pieces, q_ref, before, go_ref, taps, g_ref, ext):
-    rows, width = q_ref.shape
-    cw = width // pieces
-    rim = before.shape[1]
-    for c in range(pieces):
-        lanes = slice(c * cw, (c + 1) * cw)
-        fill(ext, before[0, :, lanes], q_ref[:, lanes], None, rim)
-        g_ref[c] = (go_ref[:, lanes].astype(F32) * short(ext, taps, rows, lanes, 0)).astype(BF16)
-
-
 def times(a, b):
     return a[0] * b[0] - a[1] * b[1], a[0] * b[1] + a[1] * b[0]
 
@@ -102,11 +93,12 @@
             spec[s, i] = out[:, p * cw : (p + 1) * cw]
 
 
-def mix_spectra(spec, primed, held):
+def mix_spectra(first, spec, held):
     count, rows2, cw = spec.shape[1:]
     half = rows2 // 2
     step = 8
     sign = 1.0 - 2.0 * (lax.broadcasted_iota(jnp.int32, (step, cw), 0) % 2).astype(F32)
+    zero = jnp.zeros((step, cw), F32)
 
     def primes(blocks):
         out = [blocks[0]]
@@ -127,54 +119,64 @@
             spec[s, i, low, :] = value[0]
             spec[s, i, high, :] = value[1]
 
-        if count <= 8:
+        def primed(s):
+            values = primes([load(s, i) for i in range(count)])
+            for i in range(count):
+                save(s, i, values[i])
+            return values
+
+        if count <= 8 and first:
+            taps = primed(1)
             mixed = [load(0, i) for i in range(count)]
-            taps = primes([load(1, i) for i in range(count)])
             for i in range(count):
                 total = None
                 for d in range(i + 1):
                     total = add(total, times(taps[d], mixed[i - d]))
-                save(0, i, total)
+                save(2, i, total)
+            return carry
+        if count <= 8:
             grads = [load(2, i) for i in range(count)]
-            for b in range(count):
-                total = None
-                for e in range(count - b):
-                    total = add(total, conj_times(taps[e], grads[b + e]))
-                save(1, b, total)
-            mixed = primes(mixed)
-            for b in range(count):
-                total = None
-                for e in range(count - b):
-                    total = add(total, conj_times(mixed[e], grads[b + e]))
-                save(2, b, total)
+            for s in (1, 0):
+                taps = [load(s, i) for i in range(count)]
+                if s == 0:
+                    taps = primes(taps)
+                for b in range(count):
+                    total = None
+                    for e in range(count - b):
+                        total = add(total, conj_times(taps[e], grads[b + e]))
+                    save(s, b, total)
             return carry
-
-        for s in range(2):
-            for d, value in enumerate(primes([load(s, i) for i in range(count)])):
-                primed[s, d, 0] = value[0]
-                primed[s, d, 1] = value[1]
-        zero = jnp.zeros((step, cw), F32)
-
-        def one(b, inner):
-            def of_y(d, total):
-                return add(total, times((primed[1, d, 0], primed[1, d, 1]), load(0, b - d)))
-
+        if first:
+            primed(1)
+
+            def one(b, inner):
+                def of_y(d, total):
+                    return add(total, times(load(1, d), load(0, b - d)))
+
+                save(2, b, lax.fori_loop(0, b + 1, of_y, (zero, zero)))
+                return inner
+
+            lax.fori_loop(0, count, one, 0)
+            return carry
+        primed(0)
+
+        def both(b, inner):
             def of_g(e, totals):
                 grad = load(2, b + e)
-                first = conj_times((primed[1, e, 0], primed[1, e, 1]), grad)
-                second = conj_times((primed[0, e, 0], primed[0, e, 1]), grad)
-                return add(totals[0], first), add(totals[1], second)
-
-            held[0, b, 0], held[0, b, 1] = lax.fori_loop(0, b + 1, of_y, (zero, zero))
-            first, second = lax.fori_loop(0, count - b, of_g, ((zero, zero), (zero, zero)))
-            held[1, b, 0], held[1, b, 1] = first
-            held[2, b, 0], held[2, b, 1] = second
+                return (
+                    add(totals[0], conj_times(load(1, e), grad)),
+                    add(totals[1], conj_times(load(0, e), grad)),
+                )
+
+            pair = lax.fori_loop(0, count - b, of_g, ((zero, zero), (zero, zero)))
+            for s in range(2):
+                held[s, b, 0], held[s, b, 1] = pair[s]
             return inner
 
-        lax.fori_loop(0, count, one, 0)
-        for s in range(3):
-            for b in range(count):
-                save(s, b, (held[s, b, 0], held[s, b, 1]))
+        lax.fori_loop(0, count, both, 0)
+        for b in range(count):
+            save(1, b, (held[0, b, 0], held[0, b, 1]))
+            save(0, b, (held[1, b, 0], held[1, b, 1]))
         return carry
 
     lax.fori_loop(0, half // step, chunk, 0)
@@ -193,30 +195,159 @@
     return [out[:, p * cw : (p + 1) * cw].astype(BF16) for p in range(len(values))]
 
 
-def conv_kernel(mh_ref, g_ref, forward, inverse, out_ref, spec, primed, held):
+def greet(axis, size, me):
+    barrier = pltpu.get_barrier_semaphore()
+    for o in range(1, size):
+        peer = lax.rem(me + o, size)
+        pl.semaphore_signal(barrier, inc=1, device_id={axis: peer}, device_id_type=MESH)
+    pl.semaphore_wait(barrier, size - 1)
+
+
+def send(source, target, send_sem, recv_sem, peer):
+    return pltpu.make_async_remote_copy(
+        src_ref=source,
+        dst_ref=target,
+        send_sem=send_sem,
+        recv_sem=recv_sem,
+        device_id={"ctx": peer},
+        device_id_type=MESH,
+    )
+
+
+def far_first(size):
+    return sorted(range(1, size), key=lambda o: abs(o - size // 2))
+
+
+def conv_kernel(q_ref, before, go_ref, taps, mh_ref, forward, inverse, y_ref, b_ref, edge_ref,
+                ext, g_tx, g_rx, y_tx, b_tx, spec, held, sent, came, edge_sem):
     count, _, rows, cw = mh_ref.shape
+    rim = before.shape[1]
+    me = lax.axis_index("ctx")
+    greet("ctx", count, me)
+    edge_rows = edge_ref.shape[0]
+    previous = lax.rem(me + count - 1, count)
+    edge = send(go_ref.at[0:edge_rows], edge_ref, edge_sem.at[0], edge_sem.at[1], previous)
+    edge.start()
+    for c in range(count):
+        lanes = slice(c * cw, (c + 1) * cw)
+        fill(ext, before[0, :, lanes], q_ref[:, lanes], None, rim)
+        g_tx[c] = (go_ref[:, lanes].astype(F32) * short(ext, taps, rows, lanes, 0)).astype(BF16)
+
+    def exchange(kind, source, target, peer):
+        return send(
+            source.at[peer], target.at[me], sent.at[kind, peer], came.at[kind, me], peer
+        )
+
+    def arrival(kind, source, target, peer):
+        return send(
+            source.at[peer], target.at[peer], sent.at[kind, peer], came.at[kind, peer], peer
+        )
+
+    peers = [lax.rem(me + o, count) for o in far_first(count)]
+    for peer in peers:
+        exchange(0, g_tx, g_rx, peer).start()
+    g_rx[me] = g_tx[me]
+
     blocks = []
     for i in range(count):
         blocks += [(mh_ref.at[i, 0], 0, i), (mh_ref.at[i, 1], 1, i)]
-    blocks += [(g_ref.at[i], 2, i) for i in range(count)]
     spectra(forward, blocks, spec)
-    mix_spectra(spec, primed, held)
-    base = (0, rows + TAIL, 2 * (rows + TAIL))
-    for s in range(3):
-        at = base[s]
-        for i in range(0, count, 2):
-            many = min(2, count - i)
-            results = back_pair(inverse, [spec[s, i + p] for p in range(many)])
-            for p, value in enumerate(results):
-                out_ref[i + p, at : at + rows, :] = value
-                if s < 2 and i + p > 0:
-                    out_ref[i + p - 1, at + rows : at + rows + TAIL, :] = value[:TAIL]
-        if s < 2:
-            out_ref[count - 1, at + rows : at + rows + TAIL, :] = jnp.zeros((TAIL, cw), BF16)
+    mix_spectra(True, spec, held)
+    for i in range(0, count, 2):
+        for p, value in enumerate(back_pair(inverse, [spec[2, i], spec[2, i + 1]])):
+            y_tx[i + p, 0:rows, :] = value
+            if i + p > 0:
+                y_tx[i + p - 1, rows : rows + TAIL, :] = value[:TAIL]
+    y_tx[count - 1, rows : rows + TAIL, :] = jnp.zeros((TAIL, cw), BF16)
+    for peer in peers:
+        exchange(1, y_tx, y_ref, peer).start()
+    y_ref[me] = y_tx[me]
+
+    for peer in peers:
+        arrival(0, g_tx, g_rx, peer).wait_recv()
+    spectra(forward, [(g_rx.at[i], 2, i) for i in range(count)], spec)
+    mix_spectra(False, spec, held)
+
+    def give(piece):
+        @pl.when(piece != me)
+        def _():
+            exchange(2, b_tx, b_ref, piece).start()
+
+        @pl.when(piece == me)
+        def _():
+            b_ref[me] = b_tx[me]
+
+    half = count // 2
+    start = lax.rem(me // 2 + half // 2, half)
+    for k in range(half):
+        at = 2 * lax.rem(start + k, half)
+        last = lax.rem(at + count - 1, count)
+        backs = back_pair(inverse, [spec[1, at], spec[1, at + 1]])
+        longs = back_pair(inverse, [spec[0, at], spec[0, at + 1]])
+        for p in range(2):
+            b_tx[at + p, 0:rows, :] = backs[p]
+            b_tx[at + p, rows + TAIL : 2 * rows + TAIL, :] = longs[p]
+        b_tx[at, rows : rows + TAIL, :] = backs[1][:TAIL]
+        head = backs[0][:TAIL]
+        b_tx[last, rows : rows + TAIL, :] = jnp.where(at == 0, jnp.zeros_like(head), head)
+        if k > 0:
+            give(last)
+        give(at)
+    give(lax.rem(2 * start + count - 1, count))
+
+    for kind, source, target in ((1, y_tx, y_ref), (2, b_tx, b_ref)):
+        for peer in peers:
+            arrival(kind, source, target, peer).wait_recv()
+    for kind, source, target in ((0, g_tx, g_rx), (1, y_tx, y_ref), (2, b_tx, b_ref)):
+        for peer in peers:
+            exchange(kind, source, target, peer).wait_send()
+    edge.wait()
+
+    @pl.when(me == count - 1)
+    def _():
+        edge_ref[...] = jnp.zeros_like(edge_ref)
+
+
+def sum_kernel(part_ref, short_ref, skip_ref, one_rx, total, two_rx, sent, came):
+    count = part_ref.shape[0]
+    cw = part_ref.shape[2]
+    tap_count = short_ref.shape[1]
+    me = lax.axis_index("ctx")
+    greet("ctx", count, me)
+    peers = [lax.rem(me + o, count) for o in far_first(count)]
+
+    def exchange(kind, source, target, peer):
+        return send(source, target.at[me], sent.at[kind, peer], came.at[kind, me], peer)
+
+    def arrival(kind, source, target, peer):
+        return send(source, target.at[peer], sent.at[kind, peer], came.at[kind, peer], peer)
+
+    for peer in peers:
+        exchange(0, part_ref.at[peer], one_rx, peer).start()
+    one_rx[me] = part_ref[me]
+    for peer in peers:
+        arrival(0, part_ref.at[peer], one_rx, peer).wait_recv()
+    value = one_rx[0]
+    for c in range(1, count):
+        value = value + one_rx[c]
+    total[...] = value
+    for peer in peers:
+        exchange(1, total, two_rx, peer).start()
+    two_rx[me] = value
+    for peer in peers:
+        arrival(1, total, two_rx, peer).wait_recv()
+    for c in range(count):
+        lanes = slice(c * cw, (c + 1) * cw)
+        for s in range(3):
+            short_ref[s, :, lanes] = two_rx[c, s * tap_count : (s + 1) * tap_count, :]
+        skip_ref[:, lanes] = two_rx[c, 3 * tap_count : 3 * tap_count + 1, :]
+    for peer in peers:
+        exchange(0, part_ref.at[peer], one_rx, peer).wait_send()
+        exchange(1, total, two_rx, peer).wait_send()
 
 
 def leave_kernel(pieces, q_ref, k_ref, v_ref, before, after, go_ref, go_after, taps, skip_ref,
-                 got_ref, dq_ref, dk_ref, dv_ref, long_ref, sums_ref, ext, go_ext, grad_ext):
+                 y_ref, b_ref, dq_ref, dk_ref, dv_ref, long_ref, sums_ref, ext, go_ext, grad_ext):
     rows, width = q_ref.shape
     cw = width // pieces
     rim = before.shape[1]
@@ -229,18 +360,18 @@
         for s, ref in enumerate((q_ref, k_ref, v_ref)):
             fill(ext.at[s], before[s, :, lanes], ref[:, lanes], after[s, :, lanes], rim)
             filtered.append(short(ext.at[s], taps, more, lanes, s))
-        fill(go_ext, jnp.zeros((rim, cw), F32), go_ref[:, lanes], go_after[:, lanes], rim)
+        fill(go_ext, jnp.zeros((rim, cw), F32), go_ref[:, lanes], go_after[0:rim, lanes], rim)
         grad_o = go_ext[PAD : PAD + more, :]
         mixed = filtered[1] * filtered[2]
         grad_y = grad_o * filtered[0]
         gain = skip_ref[:, lanes]
-        y_full = got_ref[c, 0:more, :].astype(F32) + gain * mixed
+        y_full = y_ref[c, 0:more, :].astype(F32) + gain * mixed
         at = rows + TAIL
-        grad_mixed = got_ref[c, at : at + more, :].astype(F32) + gain * grad_y
+        grad_mixed = b_ref[c, 0:more, :].astype(F32) + gain * grad_y
         grad_ext[0, 0:more, :] = grad_o * y_full
         grad_ext[1, 0:more, :] = grad_mixed * filtered[2]
         grad_ext[2, 0:more, :] = grad_mixed * filtered[1]
-        long_ref[:, lanes] = got_ref[c, 2 * at : 2 * at + rows, :].astype(F32)
+        long_ref[:, lanes] = b_ref[c, at : at + rows, :].astype(F32)
         for s, ref in enumerate((dq_ref, dk_ref, dv_ref)):
             total = None
             own = grad_ext[s, 0:rows, :]
@@ -249,10 +380,10 @@
                 total = term if total is None else total + term
                 stream = ext[s, PAD - j : PAD - j + rows, :]
                 row = s * tap_count + j
-                sums_ref[row : row + 1, lanes] = jnp.sum(own * stream, axis=0, keepdims=True)
+                sums_ref[c, row : row + 1, :] = jnp.sum(own * stream, axis=0, keepdims=True)
             ref[:, lanes] = total.astype(BF16)
         row = 3 * tap_count
-        sums_ref[row : row + 1, lanes] = jnp.sum(
+        sums_ref[c, row : row + 1, :] = jnp.sum(
             grad_y[0:rows] * mixed[0:rows], axis=0, keepdims=True
         )
 
@@ -278,6 +409,7 @@
     starts = jnp.stack([queries[:rim], keys[:rim], values[:rim]])
     before = shifted(ends, "ctx", 1)
     after = shifted(starts, "ctx", -1)
+    before, after = lax.optimization_barrier((before, after))
     ext = pltpu.VMEM((rows + 4 * PAD, cw), F32)
     shape = jax.ShapeDtypeStruct
     mh = call(
@@ -292,33 +424,38 @@
         (((1,), (1,)), ((), ())),
         preferred_element_type=F32,
     ).astype(BF16)
-    go_after = shifted(grad_o[:rim], "ctx", -1)
-    g = call(
-        functools.partial(grad_kernel, ctx),
-        shape((ctx, rows, cw), BF16), [ext],
-        queries, before, grad_o, short_filters,
-    )
-    g = lax.all_to_all(g, "ctx", split_axis=0, concat_axis=0, tiled=True)
     forward, inverse = tables(rows)
     spare = ctx if ctx > 8 else 1
-    back = call(
+    one = shape((ctx, rows + TAIL, cw), BF16)
+    two = shape((ctx, 2 * rows + TAIL, cw), BF16)
+    piece = pltpu.VMEM((ctx, rows, cw), BF16)
+    y, back, go_after = call(
         conv_kernel,
-        shape((ctx, 3 * rows + 2 * TAIL, cw), BF16),
-        [pltpu.VMEM((3, ctx, 2 * rows, cw), F32), pltpu.VMEM((2, spare, 2, 8, cw), F32),
-         pltpu.VMEM((3, spare, 2, 8, cw), F32)],
-        mh, g, jnp.asarray(forward), jnp.asarray(inverse),
-    )
-    back = lax.all_to_all(back, "ctx", split_axis=0, concat_axis=0, tiled=True)
+        (one, two, shape((TAIL, width), BF16)),
+        [ext, piece, piece, pltpu.VMEM(one.shape, BF16), pltpu.VMEM(two.shape, BF16),
+         pltpu.VMEM((3, ctx, 2 * rows, cw), F32), pltpu.VMEM((2, spare, 2, 8, cw), F32),
+         pltpu.SemaphoreType.DMA((3, ctx)), pltpu.SemaphoreType.DMA((3, ctx)),
+         pltpu.SemaphoreType.DMA((2,))],
+        queries, before, grad_o, short_filters, mh, jnp.asarray(forward), jnp.asarray(inverse),
+        collective_id=1, has_side_effects=True,
+    )
     stream = shape((rows, width), BF16)
     dq, dk, dv, d_long, sums = call(
         functools.partial(leave_kernel, ctx),
-        (stream, stream, stream, shape((rows, width), F32), shape((16, width), F32)),
+        (stream, stream, stream, shape((rows, width), F32), shape((ctx, 16, cw), F32)),
         [pltpu.VMEM((3, rows + 4 * PAD, cw), F32), ext, pltpu.VMEM((3, rows + 4 * PAD, cw), F32)],
-        queries, keys, values, before, after, grad_o, go_after, short_filters, skip[None], back,
-    )
-    sums = lax.psum(sums, "ctx")
-    d_short = sums[: 3 * tap_count].reshape(3, tap_count, width)
-    return dq, dk, dv, d_long, d_short, sums[3 * tap_count]
+        queries, keys, values, before, after, grad_o, go_after, short_filters, skip[None], y, back,
+    )
+    small = pltpu.VMEM((ctx, 16, cw), F32)
+    d_short, d_skip = call(
+        sum_kernel,
+        (shape((3, tap_count, width), F32), shape((1, width), F32)),
+        [small, pltpu.VMEM((16, cw), F32), small,
+         pltpu.SemaphoreType.DMA((2, ctx)), pltpu.SemaphoreType.DMA((2, ctx))],
+        sums,
+        collective_id=2, has_side_effects=True,
+    )
+    return dq, dk, dv, d_long, d_short, d_skip[0]
 
 
 def solution(mesh):

time: 222 us -> 147 us (0.66)
  waiting for transfers between devices: 125 us -> 22.4 us
  Pallas kernels: 24.3 us -> 80.8 us
  blocking collectives: 20.5 us -> 0 us
  starting transfers between devices: 18.2 us -> 11.9 us
    psum x1 -> x0, waiting for transfers between devices: 67.4 us -> none  [per_device(): sums = lax.psum(sums, 'ctx')]
    pallas_call x4, Pallas kernels: 24.3 us -> 80.8 us  [call(): pl.pallas_call(kernel, out_shape=out_shape, in_specs=[pl.BlockSpec(memory...]
    all_to_all x1 -> x0, waiting for transfers between devices: 29.7 us -> none  [per_device(): back = lax.all_to_all(back, 'ctx', split_axis=0, concat_axis=0, tiled=True)]
    all_to_all x1 -> x0, blocking collectives: 20.5 us -> none  [per_device(): g = lax.all_to_all(g, 'ctx', split_axis=0, concat_axis=0, tiled=True)]
    all_to_all x1 -> x0, starting transfers between devices: 3.64 us -> none  [per_device(): back = lax.all_to_all(back, 'ctx', split_axis=0, concat_axis=0, tiled=True)]
    all_gather x1, waiting for transfers between devices: 20.3 us -> 17.5 us  [per_device(): lax.all_gather(d_out, 'ch', axis=1, tiled=True)]
    ppermute x3 -> x2, waiting for transfers between devices: 6.65 us -> 4.29 us  [shifted(): return lax.ppermute(block, axis, route)]
    ppermute x3 -> x2, starting transfers between devices: 7.65 us -> 6.19 us  [shifted(): return lax.ppermute(block, axis, route)]
  transfers between devices with their start and end apart: 7 -> 4, of which waited for: 6 -> 3; matrix products, arithmetic and copies ran while one was open for 7% -> 10% of each run, Pallas kernels for 3% -> 2%
where the time goes in v2:
time: 147 us
  Pallas kernels  80.8 us (55%)
  waiting for transfers between devices  22.4 us (15%)
  between operations  14.1 us (10%)
  matrix products  12.4 us (8%)
  starting transfers between devices  11.9 us (8%)
  local copies, waits for them, and re-layouts  5.23 us (4%)
    pallas_call x4, Pallas kernels, call(): pl.pallas_call(kernel, out_shape=out_shape, in_specs=[pl.BlockSpec(memory...  80.8 us
    all_gather x1, waiting for transfers between devices, per_device(): lax.all_gather(d_out, 'ch', axis=1, tiled=True)  17.5 us
    dot_general x1, matrix products, per_device(): lax.dot_general(lax.all_gather(d_out, 'ch', axis=1, tiled=True), w_out, (...  12.4 us
    ppermute x2, starting transfers between devices, shifted(): return lax.ppermute(block, axis, route)  6.19 us
    all_to_all x1, starting transfers between devices, per_device(): mh = lax.all_to_all(mh, 'ctx', split_axis=0, concat_axis=0, tiled=True)  5.7 us
    ppermute x2, waiting for transfers between devices, shifted(): return lax.ppermute(block, axis, route)  4.29 us
    unnamed x8, local copies, waits for them, and re-layouts  3.68 us
  transfers between devices with their start and end apart: 4, of which 3 were waited for; matrix products, arithmetic and copies ran while one was open for 10% of the time, Pallas kernels for 2%

profile of v2, /device:TPU:0, one launch (start us, length us, event | category | flops | bytes accessed | tf_op | source)
XLA Modules:
  0.0 146.9 jit_solution(12438046249265360908)
XLA Ops:
  7.2 0.0 all-gather.2.cloned.1.call-start
  7.2 0.7 all-gather.2.cloned.1.call-update
  7.9 0.7 slice_bitcast_fusion.2
  8.7 0.8 slice_bitcast_fusion
  9.5 4.9 %collective-permute-start = (bf16[3,2,1024]{2,1,0:T(2,128)(2,1)S(1)}, bf16[3,2,1024]{2,1,0:T(2,128)(2,1)S(1)}, u32[]{:S(2)}, u32[]{:S(2)}) collective-permute-start(bf16[3,2,1024]{2,1,0:T(2,128)(2,1)S(1)} %pad_maximum_fusion), channel_id=1, source_target_pairs={{0,4},{4,8},{8,12},{12,16},{16,20},{20,24},{24,28},{1,5},{5,9},{9,... | collective-permute-start | bytes 36872 | tf_op jit(solution)/shard_map/ppermute | solution.py:38
  14.4 1.3 collective-permute-start.1
  15.7 0.1 collective-permute-done.before
  15.8 0.0 copy-start.1
  15.8 4.2 %collective-permute-done.1.after = bf16[3,2,1024]{2,1,0:T(2,128)(2,1)S(1)} collective-permute-done((bf16[3,2,1024]{2,1,0:T(2,128)(2,1)S(1)}, bf16[3,2,1024]{2,1,0:T(2,128)(2,1)S(1)}, u32[]{:S(2)}, u32[]{:S(2)}) %collective-permute-start.1) | collective-permute-done | bytes 12320 | tf_op jit(solution)/shard_map/ppermute | solution.py:38
  20.0 0.0 copy-done.1
  20.0 0.0 copy-start.2
  20.0 3.5 %shard_map.145 = bf16[8,2,256,128]{3,2,1,0:T(8,128)(2,1)} custom-call(bf16[256,1024]{1,0:T(8,128)(2,1)} %k_ref.3, bf16[256,1024]{1,0:T(8,128)(2,1)} %v_ref.3, bf16[3,2,1024]{2,1,0:T(2,128)(2,1)} %copy-done.1, f32[256,1024]{1,0:T(8,128)} %long_ref.1, f32[3,3,1024]{2,1,0:T(4,128)} %taps.5), custom_call_target="tpu_custom_call" | custom-call | tf_op jit(solution)/shard_map/pallas_call | solution.py:392
  23.6 5.7 %all-to-all-start = ((bf16[8,2,256,128]{3,2,1,0:T(8,128)(2,1)}), bf16[8,2,256,128]{3,2,1,0:T(8,128)(2,1)S(1)}, u32[]{:S(2)}, u32[]{:S(2)}) async-start(bf16[8,2,256,128]{3,2,1,0:T(8,128)(2,1)} %shard_map.145), calls=%async_computation | async-start | bytes 2097152 | tf_op jit(solution)/shard_map/all_to_all | solution.py:420
  29.3 17.5 %all-gather.2.cloned.1.call-done = bf16[256,8192]{1,0:T(8,128)(2,1)} async-done(((bf16[256,2048]{1,0:T(8,128)(2,1)}), bf16[256,8192]{1,0:T(8,128)(2,1)}) %all-gather.2.cloned.1.call-update) | async-done | bytes 4194320 | tf_op jit(solution)/shard_map/all_gather | solution.py:422
  46.7 12.4 %convolution_convert_fusion.go_ref = bf16[256,1024]{1,0:T(8,128)(2,1)} fusion(bf16[256,8192]{1,0:T(8,128)(2,1)} %all-gather.2.cloned.1.call-done, bf16[1024,8192]{1,0:T(8,128)(2,1)} %param.16), kind=kOutput, calls=%fused_computation | convolution fusion | flops 4295229440 | bytes 21495808 | tf_op jit(solution)/shard_map/dot_general | solution.py:421
  59.1 0.0 copy-done.2
  59.1 0.0 all-to-all-done.mh_ref
  59.1 0.0 copy-start
  59.1 1.0 copy-done
  60.1 51.8 %shard_map.146 = (bf16[8,272,128]{2,1,0:T(8,128)(2,1)}, bf16[8,528,128]{2,1,0:T(8,128)(2,1)}, bf16[16,1024]{1,0:T(8,128)(2,1)}) custom-call(bf16[256,1024]{1,0:T(8,128)(2,1)} %q_ref.3, bf16[3,2,1024]{2,1,0:T(2,128)(2,1)} %copy-done.1, bf16[256,1024]{1,0:T(8,128)(2,1)} %convolution_convert_fusion.go_ref, f32[3,3,1024]{2,1,0:T(4,128)} %taps.5, ...), custom_call_target="tpu_custom_call" | custom-call | tf_op jit(solution)/shard_map/pallas_call | solution.py:392
  111.9 7.3 %shard_map.147 = (bf16[256,1024]{1,0:T(8,128)(2,1)}, bf16[256,1024]{1,0:T(8,128)(2,1)}, bf16[256,1024]{1,0:T(8,128)(2,1)}, f32[256,1024]{1,0:T(8,128)}, f32[8,16,128]{2,1,0:T(8,128)}) custom-call(bf16[256,1024]{1,0:T(8,128)(2,1)} %q_ref.3, bf16[256,1024]{1,0:T(8,128)(2,1)} %k_ref.3, bf16[256,1024]{1,0:T(8,128)(2,1)} %v_ref.3, bf16[3,2,1024]{2,1,0:T(2,128)(2,1)} %copy-done.1, ...), custom_call_target="tpu_custom_call" | custom-call | tf_op jit(solution)/shard_map/pallas_call | solution.py:392
  119.3 18.1 %shard_map.148 = (f32[3,3,1024]{2,1,0:T(4,128)}, f32[1,1024]{1,0:T(1,128)}) custom-call(f32[8,16,128]{2,1,0:T(8,128)} %get-tuple-element.27.part_ref), custom_call_target="tpu_custom_call" | custom-call | tf_op jit(solution)/shard_map/pallas_call | solution.py:392
  137.3 1.4 copy.18
  138.7 1.3 copy.19
  (2 shorter events, 0.0 us)
Async XLA Ops:
  7.2 39.6 %all-gather.2.cloned.1.call-start = ((), (), s32[]{:S(2)}) async-start(), calls=%async_computation.1 | async-start | bytes 5242880 | tf_op jit(solution)/shard_map/all_gather | solution.py:422
  9.5 6.3 %collective-permute-start = (bf16[3,2,1024]{2,1,0:T(2,128)(2,1)S(1)}, bf16[3,2,1024]{2,1,0:T(2,128)(2,1)S(1)}, u32[]{:S(2)}, u32[]{:S(2)}) collective-permute-start(bf16[3,2,1024]{2,1,0:T(2,128)(2,1)S(1)} %pad_maximum_fusion), channel_id=1, source_target_pairs={{0,4},{4,8},{8,12},{12,16},{16,20},{20,24},{24,28},{1,5},{5,9},{9,... | collective-permute-start | bytes 36872 | tf_op jit(solution)/shard_map/ppermute | solution.py:38
  14.4 5.6 %collective-permute-start.1 = (bf16[3,2,1024]{2,1,0:T(2,128)(2,1)S(1)}, bf16[3,2,1024]{2,1,0:T(2,128)(2,1)S(1)}, u32[]{:S(2)}, u32[]{:S(2)}) collective-permute-start(bf16[3,2,1024]{2,1,0:T(2,128)(2,1)S(1)} %pad_maximum_fusion.1), channel_id=1, source_target_pairs={{4,0},{8,4},{12,8},{16,12},{20,16},{24,20},{28,24},{5,1},{9,5},{13... | collective-permute-start | bytes 36872 | tf_op jit(solution)/shard_map/ppermute | solution.py:38
  15.8 4.2 %copy-start.1 = (bf16[3,2,1024]{2,1,0:T(2,128)(2,1)}, bf16[3,2,1024]{2,1,0:T(2,128)(2,1)S(1)}, u32[]{:S(2)}) copy-start(bf16[3,2,1024]{2,1,0:T(2,128)(2,1)S(1)} %collective-permute-done.before) | copy-start | bytes 36868
  20.0 39.1 %copy-start.2 = (bf16[3,2,1024]{2,1,0:T(2,128)(2,1)}, bf16[3,2,1024]{2,1,0:T(2,128)(2,1)S(1)}, u32[]{:S(2)}) copy-start(bf16[3,2,1024]{2,1,0:T(2,128)(2,1)S(1)} %collective-permute-done.1.after) | copy-start | bytes 36868
  23.6 35.5 %all-to-all-start = ((bf16[8,2,256,128]{3,2,1,0:T(8,128)(2,1)}), bf16[8,2,256,128]{3,2,1,0:T(8,128)(2,1)S(1)}, u32[]{:S(2)}, u32[]{:S(2)}) async-start(bf16[8,2,256,128]{3,2,1,0:T(8,128)(2,1)} %shard_map.145), calls=%async_computation | async-start | bytes 2097152 | tf_op jit(solution)/shard_map/all_to_all | solution.py:420
  59.1 1.0 copy-start
Sparse Core Ops, SparseCore 0:
  9.5 37.1 all-gather.1

commit v3 on v2

--- a/solution.py
+++ b/solution.py
@@ -30,12 +30,6 @@
     angle = (2 * freq + 1) * place % (4 * block) * (math.pi / (2 * block))
     forward = np.concatenate([np.cos(angle), -np.sin(angle)], axis=0)
     return split_table(forward), split_table(forward.T / block)
-
-
-def shifted(block, axis, distance):
-    devices = range(lax.axis_size(axis))
-    route = [(i - distance, i) for i in devices if i - distance in devices]
-    return lax.ppermute(block, axis, route)
 
 
 def fill(scratch, before, own, after, rim):
@@ -54,19 +48,6 @@
         term = taps[s, j : j + 1, lanes] * scratch[PAD - j : PAD - j + rows, :]
         total = term if total is None else total + term
     return total
-
-
-def enter_kernel(pieces, k_ref, v_ref, before, long_ref, taps, mh_ref, ext):
-    rows, width = k_ref.shape
-    cw = width // pieces
-    rim = before.shape[1]
-    for c in range(pieces):
-        lanes = slice(c * cw, (c + 1) * cw)
-        fill(ext, before[1, :, lanes], k_ref[:, lanes], None, rim)
-        keyed = short(ext, taps, rows, lanes, 1)
-        fill(ext, before[2, :, lanes], v_ref[:, lanes], None, rim)
-        mh_ref[c, 0] = (keyed * short(ext, taps, rows, lanes, 2)).astype(BF16)
-        mh_ref[c, 1] = long_ref[:, lanes].astype(BF16)
 
 
 def times(a, b):
@@ -195,42 +176,158 @@
     return [out[:, p * cw : (p + 1) * cw].astype(BF16) for p in range(len(values))]
 
 
-def greet(axis, size, me):
+def greet(sizes):
     barrier = pltpu.get_barrier_semaphore()
-    for o in range(1, size):
-        peer = lax.rem(me + o, size)
-        pl.semaphore_signal(barrier, inc=1, device_id={axis: peer}, device_id_type=MESH)
-    pl.semaphore_wait(barrier, size - 1)
-
-
-def send(source, target, send_sem, recv_sem, peer):
+    for axis, size in sizes:
+        me = lax.axis_index(axis)
+        for o in range(1, size):
+            peer = lax.rem(me + o, size)
+            pl.semaphore_signal(barrier, inc=1, device_id={axis: peer}, device_id_type=MESH)
+    pl.semaphore_wait(barrier, sum(size - 1 for _, size in sizes))
+
+
+def send(source, target, send_sem, recv_sem, peer, axis="ctx"):
     return pltpu.make_async_remote_copy(
         src_ref=source,
         dst_ref=target,
         send_sem=send_sem,
         recv_sem=recv_sem,
-        device_id={"ctx": peer},
+        device_id={axis: peer},
         device_id_type=MESH,
     )
 
 
 def far_first(size):
     return sorted(range(1, size), key=lambda o: abs(o - size // 2))
+
+
+def gather_kernel(q_ref, k_ref, v_ref, long_ref, taps, d_ref, w_hbm,
+                  mh_ref, go_ref, before, after, ext, mh_tx, held, weights, total,
+                  edge_sent, edge_came, sent, came, own_sent, pass_sent, d_came, w_sem):
+    count, _, rows, cw = mh_ref.shape
+    parts, halves = held.shape[:2]
+    cols = d_ref.shape[1]
+    piece = cols // halves
+    rim = taps.shape[1] - 1
+    me = lax.axis_index("ctx")
+    mine = lax.axis_index("ch")
+    partner = mine + 1 - 2 * lax.rem(mine, 2)
+    greet([("ctx", count), ("ch", parts)])
+
+    rest = [lax.rem(mine + 2 * o, parts) for o in range(1, parts // 2)]
+    other = [lax.rem(partner + 2 * o, parts) for o in range(1, parts // 2)]
+    after_me = lax.rem(me + 1, count)
+    before_me = lax.rem(me + count - 1, count)
+
+    edges = []
+    for s, ref in ((1, k_ref), (2, v_ref), (0, q_ref)):
+        edges.append(send(ref.at[rows - TAIL : rows], before.at[s], edge_sent.at[s],
+                          edge_came.at[s], after_me))
+    for s, ref in ((0, q_ref), (1, k_ref), (2, v_ref)):
+        edges.append(send(ref.at[0:TAIL], after.at[s], edge_sent.at[3 + s],
+                          edge_came.at[3 + s], before_me))
+    for edge in edges:
+        edge.start()
+
+    def own(slot, half, peer):
+        lanes = slice(half * piece, (half + 1) * piece)
+        return send(d_ref.at[:, lanes], held.at[mine, half], own_sent.at[slot, half],
+                    d_came.at[mine, half], peer, "ch")
+
+    def passed(slot, half, part):
+        return send(held.at[part, half], held.at[part, half], pass_sent.at[slot, half],
+                    d_came.at[part, half], partner, "ch")
+
+    for half in range(halves):
+        for slot, peer in enumerate(rest + [partner]):
+            own(slot, half, peer).start()
+
+    def weight(part):
+        lanes = pl.ds(pl.multiple_of(part * cols, cols), cols)
+        return pltpu.make_async_copy(w_hbm.at[:, lanes], weights.at[part], w_sem.at[part])
+
+    order = [mine, partner] + [p for pair in zip(rest, other) for p in pair]
+    for part in order:
+        weight(part).start()
+    for edge in edges:
+        edge.wait()
+
+    @pl.when(me == 0)
+    def _():
+        before[...] = jnp.zeros_like(before)
+
+    @pl.when(me == count - 1)
+    def _():
+        after[...] = jnp.zeros_like(after)
+
+    for c in range(count):
+        lanes = slice(c * cw, (c + 1) * cw)
+        fill(ext, before[1, TAIL - rim :, lanes], k_ref[:, lanes], None, rim)
+        keyed = short(ext, taps, rows, lanes, 1)
+        fill(ext, before[2, TAIL - rim :, lanes], v_ref[:, lanes], None, rim)
+        mh_tx[c, 0] = (keyed * short(ext, taps, rows, lanes, 2)).astype(BF16)
+        mh_tx[c, 1] = long_ref[:, lanes].astype(BF16)
+
+    def exchange(peer):
+        return send(mh_tx.at[peer], mh_ref.at[me], sent.at[peer], came.at[me], peer)
+
+    def arrival(peer):
+        return send(mh_tx.at[peer], mh_ref.at[peer], sent.at[peer], came.at[peer], peer)
+
+    peers = [lax.rem(me + o, count) for o in far_first(count)]
+    for peer in peers:
+        exchange(peer).start()
+    mh_ref[me] = mh_tx[me]
+
+    def product(data, part, half=None):
+        lanes = slice(None) if half is None else slice(half * piece, (half + 1) * piece)
+        return lax.dot_general(data, weights[part, :, lanes], (((1,), (1,)), ((), ())),
+                               preferred_element_type=F32)
+
+    def take(part, half):
+        total[...] += product(held[part, half], part, half)
+
+    weight(mine).wait()
+    total[...] = product(d_ref[...], mine)
+    weight(partner).wait()
+    for half in range(halves):
+        passed(0, half, partner).wait_recv()
+        take(partner, half)
+    for slot, (direct, relayed) in enumerate(zip(rest, other)):
+        weight(direct).wait()
+        weight(relayed).wait()
+        for half in range(halves):
+            passed(slot, half, direct).wait_recv()
+            passed(slot, half, direct).start()
+            take(direct, half)
+            passed(slot, half, relayed).wait_recv()
+            take(relayed, half)
+    go_ref[...] = total[...].astype(BF16)
+
+    for peer in peers:
+        arrival(peer).wait_recv()
+    for peer in peers:
+        exchange(peer).wait_send()
+    for half in range(halves):
+        for slot, peer in enumerate(rest + [partner]):
+            own(slot, half, peer).wait_send()
+        for slot, direct in enumerate(rest):
+            passed(slot, half, direct).wait_send()
 
 
 def conv_kernel(q_ref, before, go_ref, taps, mh_ref, forward, inverse, y_ref, b_ref, edge_ref,
                 ext, g_tx, g_rx, y_tx, b_tx, spec, held, sent, came, edge_sem):
     count, _, rows, cw = mh_ref.shape
-    rim = before.shape[1]
+    rim = taps.shape[1] - 1
     me = lax.axis_index("ctx")
-    greet("ctx", count, me)
+    greet([("ctx", count)])
     edge_rows = edge_ref.shape[0]
     previous = lax.rem(me + count - 1, count)
     edge = send(go_ref.at[0:edge_rows], edge_ref, edge_sem.at[0], edge_sem.at[1], previous)
     edge.start()
     for c in range(count):
         lanes = slice(c * cw, (c + 1) * cw)
-        fill(ext, before[0, :, lanes], q_ref[:, lanes], None, rim)
+        fill(ext, before[0, TAIL - rim :, lanes], q_ref[:, lanes], None, rim)
         g_tx[c] = (go_ref[:, lanes].astype(F32) * short(ext, taps, rows, lanes, 0)).astype(BF16)
 
     def exchange(kind, source, target, peer):
@@ -313,7 +410,7 @@
     cw = part_ref.shape[2]
     tap_count = short_ref.shape[1]
     me = lax.axis_index("ctx")
-    greet("ctx", count, me)
+    greet([("ctx", count)])
     peers = [lax.rem(me + o, count) for o in far_first(count)]
 
     def exchange(kind, source, target, peer):
@@ -350,7 +447,7 @@
                  y_ref, b_ref, dq_ref, dk_ref, dv_ref, long_ref, sums_ref, ext, go_ext, grad_ext):
     rows, width = q_ref.shape
     cw = width // pieces
-    rim = before.shape[1]
+    rim = taps.shape[1] - 1
     tap_count = taps.shape[1]
     more = rows + PAD
     sums_ref[...] = jnp.zeros_like(sums_ref)
@@ -358,7 +455,7 @@
         lanes = slice(c * cw, (c + 1) * cw)
         filtered = []
         for s, ref in enumerate((q_ref, k_ref, v_ref)):
-            fill(ext.at[s], before[s, :, lanes], ref[:, lanes], after[s, :, lanes], rim)
+            fill(ext.at[s], before[s, TAIL - rim :, lanes], ref[:, lanes], after[s, 0:rim, lanes], rim)
             filtered.append(short(ext.at[s], taps, more, lanes, s))
         fill(go_ext, jnp.zeros((rim, cw), F32), go_ref[:, lanes], go_after[0:rim, lanes], rim)
         grad_o = go_ext[PAD : PAD + more, :]
@@ -388,12 +485,14 @@
         )
 
 
-def call(kernel, out_shape, scratch, *args, **params):
+def call(kernel, out_shape, scratch, *args, hbm=(), **params):
+    vmem = pl.BlockSpec(memory_space=pltpu.VMEM)
     return pl.pallas_call(
         kernel,
         out_shape=out_shape,
-        in_specs=[pl.BlockSpec(memory_space=pltpu.VMEM)] * len(args),
-        out_specs=jax.tree.map(lambda _: pl.BlockSpec(memory_space=pltpu.VMEM), out_shape),
+        in_specs=[pl.BlockSpec(memory_space=pl.ANY) if i in hbm else vmem
+                  for i in range(len(args))],
+        out_specs=jax.tree.map(lambda _: vmem, out_shape),
         scratch_shapes=scratch,
         compiler_params=pltpu.CompilerParams(**PARAMS, **params),
     )(*args)
@@ -404,26 +503,24 @@
     rows, width = queries.shape
     cw = width // ctx
     tap_count = short_filters.shape[1]
-    rim = tap_count - 1
-    ends = jnp.stack([queries[rows - rim :], keys[rows - rim :], values[rows - rim :]])
-    starts = jnp.stack([queries[:rim], keys[:rim], values[:rim]])
-    before = shifted(ends, "ctx", 1)
-    after = shifted(starts, "ctx", -1)
-    before, after = lax.optimization_barrier((before, after))
+    parts = lax.axis_size("ch")
+    cols = d_out.shape[1]
+    halves = 2
     ext = pltpu.VMEM((rows + 4 * PAD, cw), F32)
     shape = jax.ShapeDtypeStruct
-    mh = call(
-        functools.partial(enter_kernel, ctx),
-        shape((ctx, 2, rows, cw), BF16), [ext],
-        keys, values, before, long_filter, short_filters,
-    )
-    mh = lax.all_to_all(mh, "ctx", split_axis=0, concat_axis=0, tiled=True)
-    grad_o = lax.dot_general(
-        lax.all_gather(d_out, "ch", axis=1, tiled=True),
-        w_out,
-        (((1,), (1,)), ((), ())),
-        preferred_element_type=F32,
-    ).astype(BF16)
+    dma = pltpu.SemaphoreType.DMA
+    edge = shape((3, TAIL, width), BF16)
+    pair = (ctx, 2, rows, cw)
+    mh, grad_o, before, after = call(
+        gather_kernel,
+        (shape(pair, BF16), shape((rows, width), BF16), edge, edge),
+        [ext, pltpu.VMEM(pair, BF16), pltpu.VMEM((parts, halves, rows, cols // halves), BF16),
+         pltpu.VMEM((parts, width, cols), BF16), pltpu.VMEM((rows, width), F32),
+         dma((6,)), dma((6,)), dma((ctx,)), dma((ctx,)), dma((parts // 2, halves)),
+         dma((parts // 2, halves)), dma((parts, halves)), dma((parts,))],
+        queries, keys, values, long_filter, short_filters, d_out, w_out,
+        hbm=(6,), collective_id=3, has_side_effects=True,
+    )
     forward, inverse = tables(rows)
     spare = ctx if ctx > 8 else 1
     one = shape((ctx, rows + TAIL, cw), BF16)

time: 147 us -> 119 us (0.81)
  Pallas kernels: 80.8 us -> 115 us
  waiting for transfers between devices: 22.4 us -> 0 us
  between operations: 14.1 us -> 0.66 us
  matrix products: 12.4 us -> 0 us
  starting transfers between devices: 11.9 us -> 0 us
  local copies, waits for them, and re-layouts: 5.23 us -> 2.7 us
    pallas_call x4, Pallas kernels: 80.8 us -> 115 us  [call(): pl.pallas_call(kernel, out_shape=out_shape, in_specs=[pl.BlockSpec(memory...]
    all_gather x1 -> x0, waiting for transfers between devices: 17.5 us -> none  [per_device(): lax.all_gather(d_out, 'ch', axis=1, tiled=True)]
    dot_general x1 -> x0, matrix products: 12.4 us -> none  [per_device(): lax.dot_general(lax.all_gather(d_out, 'ch', axis=1, tiled=True), w_out, (...]
    ppermute x2 -> x0, starting transfers between devices: 6.19 us -> none  [shifted(): return lax.ppermute(block, axis, route)]
    all_to_all x1 -> x0, starting transfers between devices: 5.7 us -> none  [per_device(): mh = lax.all_to_all(mh, 'ctx', split_axis=0, concat_axis=0, tiled=True)]
    ppermute x2 -> x0, waiting for transfers between devices: 4.29 us -> none  [shifted(): return lax.ppermute(block, axis, route)]
    another operation x2 -> x0, local copies, waits for them, and re-layouts: 1.56 us -> none  [per_device(): starts = jnp.stack([queries[:rim], keys[:rim], values[:rim]])]
    unnamed x8 -> x2, local copies, waits for them, and re-layouts: 3.68 us -> 2.7 us
  transfers between devices with their start and end apart: 4 -> 0, of which waited for: 3 -> 0; matrix products, arithmetic and copies ran while one was open for 10% -> 0% of each run, Pallas kernels for 2% -> 0%
where the time goes in v3:
time: 119 us; the launch traced here: 118 us
  Pallas kernels  115 us (97%)
  local copies, waits for them, and re-layouts  2.7 us (2%)
    pallas_call x4, Pallas kernels, call(): pl.pallas_call(kernel, out_shape=out_shape, in_specs=[pl.BlockSpec(memory...  115 us
    unnamed x2, local copies, waits for them, and re-layouts  2.7 us

profile of v3, /device:TPU:0, one launch (start us, length us, event | category | flops | bytes accessed | tf_op | source)
XLA Modules:
  0.0 118.4 jit_solution(6493785437932307448)
XLA Ops:
  0.6 35.7 %shard_map.145 = (bf16[8,2,256,128]{3,2,1,0:T(8,128)(2,1)}, bf16[256,1024]{1,0:T(8,128)(2,1)}, bf16[3,16,1024]{2,1,0:T(8,128)(2,1)}, bf16[3,16,1024]{2,1,0:T(8,128)(2,1)}) custom-call(bf16[256,1024]{1,0:T(8,128)(2,1)} %q_ref.5, bf16[256,1024]{1,0:T(8,128)(2,1)} %k_ref.3, bf16[256,1024]{1,0:T(8,128)(2,1)} %v_ref.3, f32[256,1024]{1,0:T(8,128)} %long_ref.1, ...), custom_call_target="tpu_custom_call" | custom-call | tf_op jit(solution)/shard_map/pallas_call | solution.py:490
  36.3 51.6 %shard_map.146 = (bf16[8,272,128]{2,1,0:T(8,128)(2,1)}, bf16[8,528,128]{2,1,0:T(8,128)(2,1)}, bf16[16,1024]{1,0:T(8,128)(2,1)}) custom-call(bf16[256,1024]{1,0:T(8,128)(2,1)} %q_ref.5, bf16[3,16,1024]{2,1,0:T(8,128)(2,1)} %get-tuple-element.20.before, bf16[256,1024]{1,0:T(8,128)(2,1)} %get-tuple-element.22.go_ref, f32[3,3,1024]{2,1,0:T(4,128)} %taps.5, ...), custom_call_target="tpu_custom_call" | custom-call | tf_op jit(solution)/shard_map/pallas_call | solution.py:490
  87.9 7.4 %shard_map.147 = (bf16[256,1024]{1,0:T(8,128)(2,1)}, bf16[256,1024]{1,0:T(8,128)(2,1)}, bf16[256,1024]{1,0:T(8,128)(2,1)}, f32[256,1024]{1,0:T(8,128)}, f32[8,16,128]{2,1,0:T(8,128)}) custom-call(bf16[256,1024]{1,0:T(8,128)(2,1)} %q_ref.5, bf16[256,1024]{1,0:T(8,128)(2,1)} %k_ref.3, bf16[256,1024]{1,0:T(8,128)(2,1)} %v_ref.3, ...), custom_call_target="tpu_custom_call" | custom-call | tf_op jit(solution)/shard_map/pallas_call | solution.py:490
  95.3 20.4 %shard_map.148 = (f32[3,3,1024]{2,1,0:T(4,128)}, f32[1,1024]{1,0:T(1,128)}) custom-call(f32[8,16,128]{2,1,0:T(8,128)} %get-tuple-element.31.part_ref), custom_call_target="tpu_custom_call" | custom-call | tf_op jit(solution)/shard_map/pallas_call | solution.py:490
  115.7 1.4 %copy.18 = f32[3,3,1024]{2,1,0:T(4,128)} copy(f32[3,3,1024]{2,1,0:T(4,128)} %get-tuple-element.44) | data formatting | bytes 73728
  117.1 1.3 %copy.19 = f32[1024]{0:T(1024)} copy(f32[1024]{0:T(1024)} %bitcast.3) | data formatting | bytes 8192
